TPU v7x, 128 devices: a whole 4x4x4 slice. The times are simulated.
128 devices in a mesh: pair: 4 (over z_lo, core), shot: 32 (over x, y, z_hi).
Axes of the slice: x: 4, y: 4, z: 4 (z_hi: 2, z_lo: 2; z = z_hi * 2 + z_lo), core: 2. Of those that a mesh axis runs over, the one named last changes fastest.
Arguments:
- records: bfloat16 [8, 768, 768, 128], P('pair', 'shot'), may hold values from -6 to 6
- surface: float32 [32, 768], P('shot'), may hold values from 0.4 to 1.2
- mirror: int32 [8], replicated, may hold values from 0 to 7, as said below
Outputs:
- predicted: bfloat16 [8, 768, 768, 128], P('pair', 'shot')
Inputs may be any that keep to these rules, and one draw needn't show every extreme that they name: mirror is an involution without fixed points: mirror[mirror[g]] = g and mirror[g] differs from g for every group.
All inputs are finite; a program needn't handle non-finite values.
Results may differ from a plain program's by a relative error of at most 0.0088.
Values may be sent and summed in bfloat16 or wider, within the bound.
No kernel may reach another device: no remote copies, remote signals or barrier semaphores. Data moves between devices by JAX's collectives and lax.ppermute only.
A program may use at most 128 MiB of HBM per device.

v0:
```python
import math

import jax
import jax.numpy as jnp
from jax import lax
from jax.sharding import PartitionSpec as P

ORDERS = 2


def make_tables(freqs, time):
    product = (
        jnp.arange(1, freqs + 1, dtype=jnp.int32)[:, None]
        * jnp.arange(time, dtype=jnp.int32)[None, :]
        % time
    )
    phase = product.astype(jnp.float32) * (2.0 * math.pi / time)
    cosine = jnp.cos(phase)
    sine = jnp.sin(phase)
    forward = (jnp.stack([cosine, -sine], axis=1) * math.sqrt(2.0 / time)).astype(jnp.bfloat16)
    inverse = (jnp.stack([cosine, -sine], axis=1) / math.sqrt(freqs)).astype(jnp.bfloat16)
    return (forward, inverse)


def batch_dot(left, right):
    return jnp.einsum("kij,kjl->kil", left, right, preferred_element_type=jnp.float32)


def chain_products(own_spec, mate_spec, scale):
    mate_re = mate_spec[:, 0]
    mate_im = mate_spec[:, 1]
    column_scale = scale[:, None, None, :]
    left = (own_spec.astype(jnp.float32) * column_scale).astype(jnp.bfloat16)
    total = jnp.zeros(own_spec.shape, jnp.float32)
    for order_index in range(ORDERS):
        real_part = batch_dot(left[:, 0], mate_re) - batch_dot(left[:, 1], mate_im)
        imag_part = batch_dot(left[:, 0], mate_im) + batch_dot(left[:, 1], mate_re)
        product = jnp.stack([real_part, imag_part], axis=1)
        total = total + product
        if order_index + 1 < ORDERS:
            left = (product * column_scale).astype(jnp.bfloat16)
    return total.astype(jnp.bfloat16)


def local(records, surface, mirror):
    shot_count = lax.axis_size("shot")
    freqs = surface.shape[0] * shot_count
    time = records.shape[-1]
    receivers = records.shape[2]
    local_groups = records.shape[0]
    forward, inverse = make_tables(freqs, time)
    spectra = jnp.einsum(
        "kct,gsrt->gkcsr", forward, records, preferred_element_type=jnp.float32
    ).astype(jnp.bfloat16)
    first_group = lax.axis_index("pair") * local_groups
    target = lax.dynamic_slice_in_dim(mirror, first_group, local_groups, 0)
    own_spec = lax.all_to_all(spectra, "shot", split_axis=1, concat_axis=3, tiled=True)
    piece = lax.all_gather(own_spec, "pair", axis=0, tiled=True)
    index = jnp.arange(piece.shape[0], dtype=jnp.int32)
    onehot = (target[:, None] == index[None, :]).astype(jnp.bfloat16)
    flat = piece.reshape((piece.shape[0], -1))
    chosen = jnp.dot(onehot, flat, preferred_element_type=jnp.float32)
    mate_spec = chosen.astype(jnp.bfloat16).reshape(jnp.zeros_like(own_spec).shape)
    scale = -surface / math.sqrt(2.0 * receivers)
    merged_shape = (-1,) + own_spec.shape[2:]
    total = chain_products(
        own_spec.reshape(merged_shape),
        mate_spec.reshape(merged_shape),
        jnp.tile(scale, (local_groups, 1)),
    )
    total = total.reshape(own_spec.shape)
    return jnp.einsum(
        "gkcsr,kct->gsrt",
        lax.all_to_all(total, "shot", split_axis=3, concat_axis=1, tiled=True),
        inverse,
        preferred_element_type=jnp.float32,
    ).astype(jnp.bfloat16)


def solution(mesh):
    return jax.shard_map(
        local,
        mesh=mesh,
        in_specs=(P("pair", "shot", None, None), P("shot", None), P()),
        out_specs=P("pair", "shot", None, None),
        check_vma=False,
    )
```

profile of v0, /device:TPU:1, one launch (start us, length us, event | category | flops | bytes accessed | tf_op | source)
XLA Modules:
  0.0 426.5 jit_solution(15133419984614612505)
XLA Ops:
  6.7 7.1 %convert_bitcast_fusion = bf16[2,32,2,24,768]{4,1,3,0,2:T(8,128)(2,1)S(1)} fusion(bf16[2,24,768,128]{3,2,1,0:T(8,128)(2,1)} %param.3, f32[32,1,128]{2,0,1:T(8,128)S(1)} %get-tuple-element.10, f32[32,1,128]{2,0,1:T(8,128)S(1)} %get-tuple-element.9), kind=kOutput, calls=%fused_computation.15 | convolution fusion | flops 606363648 | bytes 14188544 | tf_op jit(solution)/shard_map/kct,gsrt->gkcsr/dot_general | solution.py:52
  13.8 2.6 copy.20
  16.4 68.1 %all_to_all.36 = bf16[2,32,2,24,768]{4,3,0,2,1:T(8,128)(2,1)S(1)} all-to-all(bf16[2,32,2,24,768]{4,3,0,2,1:T(8,128)(2,1)S(1)} %copy.20), channel_id=1, replica_groups=mesh['pair'=4,'shot'=32] {'shot'}, dimensions={1} | all-to-all | bytes 9437184 | tf_op jit(solution)/shard_map/all_to_all | solution.py:57
  84.5 2.5 copy.21
  87.0 0.6 copy-done.2
  87.8 5.4 %fusion.4 = bf16[2,2,768,768]{3,2,0,1:T(8,128)(2,1)} fusion(f32[768]{0:T(1024)S(1)} %multiply_reduce_fusion, bf16[2,32,2,24,768]{4,3,1,2,0:T(8,128)(2,1)} %copy.21), kind=kLoop, calls=%fused_computation.9 | loop fusion | flops 7077888 | bytes 9440256 | tf_op jit(solution)/shard_map/convert_element_type | solution.py:33
  93.1 162.9 %all-gather.2.cloned.1.call-done = bf16[8,1,2,768,768]{4,3,2,1,0:T(8,128)(2,1)} async-done(((bf16[2,1,2,768,768]{4,3,2,1,0:T(8,128)(2,1)}), bf16[8,1,2,768,768]{4,3,2,1,0:T(8,128)(2,1)}) %all-gather.2.cloned.1.call-update) | async-done | bytes 18874384 | tf_op jit(solution)/shard_map/all_gather | solution.py:58
  256.0 20.1 %copy.36 = bf16[1,8,1536,768]{3,1,2,0:T(8,128)(2,1)} copy(bf16[1,8,1536,768]{3,2,1,0:T(8,128)(2,1)} %bitcast.111) | data formatting | bytes 37748736
  276.1 9.5 %convolution_convert_fusion = bf16[2,1179648]{1,0:T(2,128)(2,1)S(1)} fusion(bf16[8,1179648]{1,0:T(8,128)(2,1)} %bitcast.97, s32[2]{0:T(128)S(1)} %dynamic_slice.3), kind=kOutput, calls=%fused_computation | convolution fusion | flops 40108048 | bytes 23592968 | tf_op jit(solution)/shard_map/dot_general | solution.py:62
  285.6 0.6 copy.37
  286.2 1.7 copy-done
  287.9 4.1 fusion.10
  292.1 4.2 fusion.11
  296.2 4.2 fusion.9
  300.4 13.1 %add_bitcast_fusion.1 = (f32[2,1,768,768]{3,2,0,1:T(8,128)}, f32[2,1,1,768,768]{4,3,0,2,1:T(8,128)S(1)}, f32[2,1,1,768,768]{4,3,0,2,1:T(8,128)}, f32[2,1,768,768]{3,2,0,1:T(8,128)}) fusion(f32[2,768,768]{2,1,0:T(8,128)} %fusion.9, f32[2,768,768]{2,1,0:T(8,128)} %fusion.11, f32[2,768,768]{2,1,0:T(8,128)} %fusion.10, ...), kind=kOutput, calls=%fused_computation.30 | convolution fusion | flops 1814298624 | bytes 37748736 | tf_op jit(solution)/shard_map/kij,kjl->kil/dot_general | solution.py:26
  313.5 4.6 %fusion.1 = bf16[2,2,768,768]{3,2,0,1:T(8,128)(2,1)S(1)} fusion(f32[2,1,768,768]{3,2,0,1:T(8,128)} %get-tuple-element.7, f32[2,1,768,768]{3,2,0,1:T(8,128)} %get-tuple-element.12, f32[768]{0:T(1024)S(1)} %multiply_reduce_fusion), kind=kLoop, calls=%fused_computation.5 | loop fusion | flops 7077888 | bytes 14158848 | tf_op jit(solution)/shard_map/convert_element_type | solution.py:41
  318.1 2.0 fusion.14
  320.1 4.2 fusion.13
  324.3 2.1 subtract_bitcast_fusion
  326.3 4.7 %add_bitcast_fusion = f32[2,1,1,768,768]{4,3,0,2,1:T(8,128)S(1)} fusion(f32[2,768,768]{2,1,0:T(8,128)} %fusion.13, bf16[2,2,768,768]{3,2,0,1:T(8,128)(2,1)S(1)} %fusion.1, bf16[2,2,768,768]{3,2,1,0:T(8,128)(2,1)S(1)} %bitcast.107), kind=kOutput, calls=%fused_computation.13 | convolution fusion | flops 1813118976 | bytes 14155776 | tf_op jit(solution)/shard_map/kij,kjl->kil/dot_general | solution.py:26
  331.1 2.9 fusion
  334.0 9.3 %copy.26 = bf16[2,1,2,768,768]{4,0,2,1,3:T(2,128)(2,1)} copy(bf16[2,1,2,768,768]{4,3,0,2,1:T(8,128)(2,1)} %fusion) | data formatting | bytes 9437184 | tf_op jit(solution)/shard_map/convert_element_type | solution.py:42
  343.3 66.8 %all_to_all.37 = bf16[2,1,2,768,768]{4,0,2,1,3:T(2,128)(2,1)S(1)} all-to-all(bf16[2,1,2,768,768]{4,0,2,1,3:T(2,128)(2,1)} %copy.26), channel_id=1, replica_groups=mesh['pair'=4,'shot'=32] {'shot'}, dimensions={3} | all-to-all | bytes 9437184 | tf_op jit(solution)/shard_map/all_to_all | solution.py:74
  410.2 9.5 %bitcast_convert_fusion = bf16[2,24,768,128]{3,2,1,0:T(8,128)(2,1)} fusion(bf16[2,1,2,32,24,768]{5,0,2,4,3,1:T(2,128)(2,1)S(1)} %bitcast.99, f32[32,1,128]{2,0,1:T(8,128)S(1)} %get-tuple-element.10, f32[32,1,128]{2,0,1:T(8,128)S(1)} %get-tuple-element.9), kind=kOutput, calls=%fused_computation.1 | convolution fusion | flops 608722944 | bytes 14188544 | tf_op jit(solution)/shard_map/gkcsr,kct->gsrt/dot_general | solution.py:72
  (15 shorter events, 0.3 us)
Async XLA Ops:
  6.5 249.5 %all-gather.2.cloned.1.call-start = ((), (), s32[]{:S(2)}) async-start(), calls=%async_computation.2 | async-start | bytes 23592960 | tf_op jit(solution)/shard_map/all_gather | solution.py:58
  87.0 0.7 copy-start.2
  87.0 0.7 copy-start.1
  285.6 2.3 copy-start
  324.3 6.8 %slice-start = ((s8[4718592]{0:T(1024)(128)(4,1)}), s8[4194304]{0:T(1024)(128)(4,1)S(1)}, s32[]{:S(2)}) async-start(s8[4718592]{0:T(1024)(128)(4,1)} %bitcast.109), calls=%async_computation.3 | async-start | bytes 8388608
  326.3 4.8 %slice-start.1 = ((s8[4718592]{0:T(1024)(128)(4,1)}), s8[524288]{0:T(1024)(128)(4,1)S(1)}, s32[]{:S(2)}) async-start(s8[4718592]{0:T(1024)(128)(4,1)} %bitcast.109), calls=%async_computation.4 | async-start | bytes 1048576
Sparse Core Ops, SparseCore 0:
  87.2 168.8 all-gather.1
where the time goes:
time: 427 us; the launch traced here: 426 us
  waiting for transfers between devices  163 us (38%)
  blocking collectives  135 us (32%)
  matrix products  64.6 us (15%)
  local copies, waits for them, and re-layouts  37.6 us (9%)
  between operations  13.5 us (3%)
  other arithmetic  13 us (3%)
    all_gather x1, waiting for transfers between devices, local(): piece = lax.all_gather(own_spec, 'pair', axis=0, tiled=True)  163 us
    all_to_all x1, blocking collectives, local(): lax.all_to_all(spectra, 'shot', split_axis=1, concat_axis=3, tiled=True)  68.1 us
    all_to_all x1, blocking collectives, local(): lax.all_to_all(total, 'shot', split_axis=3, concat_axis=1, tiled=True)  66.8 us
    dot_general x8, matrix products, batch_dot(): jnp.einsum('kij,kjl->kil', left, right, preferred_element_type=jnp.float32)  38.5 us
    unnamed x12, local copies, waits for them, and re-layouts  23.1 us
    dot_general x1, matrix products, local(): jnp.einsum('gkcsr,kct->gsrt', lax.all_to_all(total, 'shot', split_axis=3,...  9.49 us
    dot_general x1, matrix products, local(): chosen = jnp.dot(onehot, flat, preferred_element_type=jnp.float32)  9.46 us
    convert_element_type x1, local copies, waits for them, and re-layouts, chain_products(): return total.astype(jnp.bfloat16)  9.32 us
  transfers between devices with their start and end apart: 1, of which 1 were waited for; matrix products, arithmetic and copies ran while one was open for 1% of the time, Pallas kernels for 0%

commit v1 on v0

v1 whole, which is shorter than its diff:
```python
import math

import jax
import jax.numpy as jnp
from jax import lax
from jax.experimental import pallas as pl
from jax.experimental.pallas import tpu as pltpu
from jax.sharding import Mesh
from jax.sharding import PartitionSpec as P

COLUMN = ("x", "y", "zh", "zl")
ROWS = 256


def make_tables(freqs, time):
    product = (
        jnp.arange(1, freqs + 1, dtype=jnp.int32)[:, None]
        * jnp.arange(time, dtype=jnp.int32)[None, :]
        % time
    )
    phase = product.astype(jnp.float32) * (2.0 * math.pi / time)
    cosine = jnp.cos(phase)
    sine = jnp.sin(phase)
    forward = (jnp.stack([cosine, -sine], axis=1) * math.sqrt(2.0 / time)).astype(jnp.bfloat16)
    inverse = (jnp.stack([cosine, -sine], axis=1) / math.sqrt(freqs)).astype(jnp.bfloat16)
    return (forward, inverse)


def deal(mirror):
    groups = mirror.shape[0]
    half = groups // 2
    index = jnp.arange(groups, dtype=jnp.int32)
    chip = index // half
    local = index % half
    within = (mirror // half) == chip
    crossing = groups - jnp.sum(within.astype(jnp.int32))
    low = jnp.minimum(index, mirror)
    color = jnp.where(
        crossing == groups,
        low >= half // 2,
        jnp.where(crossing == groups // 2, ~within, (local != 0) & (mirror % half != 0)),
    ).astype(jnp.int32)
    key = jnp.where(within, index, low)
    before = (
        (chip[:, None] == chip[None, :])
        & (color[:, None] == color[None, :])
        & (key[None, :] < key[:, None])
    )
    place = 2 * color + jnp.sum(before.astype(jnp.int32), axis=1)
    mixed = jnp.stack([crossing == groups, crossing >= groups // 2]).astype(jnp.int32)
    return place, mixed


def chain_body(scale_ref, own_ref, mate_ref, out_ref):
    scale = -scale_ref[...] / math.sqrt(2.0 * scale_ref.shape[-1])
    mate_re = mate_ref[0, 0]
    mate_im = mate_ref[0, 1]

    def dot(a, b):
        return jnp.dot(a, b, preferred_element_type=jnp.float32)

    def times(left_re, left_im):
        real = dot(left_re, mate_re) - dot(left_im, mate_im)
        imag = dot(left_re, mate_im) + dot(left_im, mate_re)
        return real, imag

    def scaled(part):
        return (part * scale).astype(jnp.bfloat16)

    real_1, imag_1 = times(
        scaled(own_ref[0, 0].astype(jnp.float32)), scaled(own_ref[0, 1].astype(jnp.float32))
    )
    real_2, imag_2 = times(scaled(real_1), scaled(imag_1))
    out_ref[0, 0] = (real_1 + real_2).astype(jnp.bfloat16)
    out_ref[0, 1] = (imag_1 + imag_2).astype(jnp.bfloat16)


def chain(pair, surface):
    members, parts, shots, recv = pair.shape
    rows = ROWS
    return pl.pallas_call(
        chain_body,
        grid=(members, shots // rows),
        in_specs=[
            pl.BlockSpec((1, recv), lambda j, m: (0, 0)),
            pl.BlockSpec((1, parts, rows, recv), lambda j, m: (j, 0, m, 0)),
            pl.BlockSpec((1, parts, shots, recv), lambda j, m: (1 - j, 0, 0, 0)),
        ],
        out_specs=pl.BlockSpec((1, parts, rows, recv), lambda j, m: (j, 0, m, 0)),
        out_shape=jax.ShapeDtypeStruct(pair.shape, jnp.bfloat16),
        compiler_params=pltpu.CompilerParams(vmem_limit_bytes=56 << 20),
    )(surface, pair, pair)


def pick(stack, where, axis):
    return [lax.dynamic_index_in_dim(stack, w, axis, keepdims=True) for w in where]


def other_core(part):
    return lax.ppermute(part, "core", [(0, 1), (1, 0)])


def local(records, surface, mirror):
    core = lax.axis_index("core")
    chip = lax.axis_index("zl")
    groups, shots, recv, time = records.shape
    freqs = lax.axis_size("x") * lax.axis_size("y") * lax.axis_size("zh")
    width = recv // 2
    forward, inverse = make_tables(freqs, time)
    place, mixed = deal(mirror)
    place = lax.dynamic_slice_in_dim(place, 2 * groups * chip, 2 * groups, 0)
    mixed = lax.dynamic_index_in_dim(mixed, chip, 0, keepdims=False)
    slots = jnp.arange(2 * groups, dtype=jnp.int32)
    order = jnp.sum(jnp.where(place[None, :] == slots[:, None], slots[None, :], 0), axis=1)

    def halves(whole, axis):
        kept = lax.dynamic_slice_in_dim(whole, core * width, width, axis)
        sent = lax.dynamic_slice_in_dim(whole, (1 - core) * width, width, axis)
        return kept, sent

    spectra = jnp.einsum(
        "kct,gsrt->kgcsr", forward, records, preferred_element_type=jnp.float32
    ).astype(jnp.bfloat16)
    kept, sent = halves(spectra, 4)
    both = jnp.concatenate([kept, other_core(sent)], axis=1)
    where = [
        jnp.where(order[i] // 2 == core, order[i] % 2, 2 + order[i] % 2) for i in range(2 * groups)
    ]
    chunks = jnp.concatenate(pick(both, where, 1), axis=1)
    chunks = chunks.reshape((2 * freqs, 2, 2, shots, width))
    chunks = lax.all_to_all(chunks, COLUMN, 0, 0, tiled=True)
    chunks = chunks.reshape((freqs, 4, 2, shots, width))

    def member(unit, j):
        return jnp.where(mixed == 1, 2 * j + unit, 2 * unit + j)

    kept = jnp.concatenate(pick(chunks, [member(core, j) for j in range(2)], 1), axis=1)
    sent = jnp.concatenate(pick(chunks, [member(1 - core, j) for j in range(2)], 1), axis=1)
    got = other_core(sent)
    first = jnp.where(core == 0, kept, got)
    second = jnp.where(core == 0, got, kept)
    pair = jnp.concatenate([first, second], axis=4)
    pair = pair.transpose(1, 2, 0, 3, 4).reshape((2, 2, freqs * shots, recv))

    total = chain(pair, surface)

    kept, sent = halves(total, 3)
    both = jnp.concatenate([kept, other_core(sent)], axis=0)
    both = both.reshape((4, 2, freqs, shots, width))
    where = []
    for i in range(4):
        unit = jnp.where(mixed == 1, i % 2, i // 2)
        j = jnp.where(mixed == 1, i // 2, i % 2)
        where.append(jnp.where(unit == core, j, 2 + j))
    chunks = jnp.concatenate(pick(both, where, 0), axis=0).transpose(2, 0, 1, 3, 4)
    chunks = chunks.reshape((2 * freqs, 2, 2, shots, width))
    chunks = lax.all_to_all(chunks, COLUMN, 0, 0, tiled=True)
    chunks = chunks.reshape((freqs, 4, 2, shots, width))
    kept = jnp.concatenate(pick(chunks, [place[2 * core + g] for g in range(groups)], 1), axis=1)
    sent = jnp.concatenate(
        pick(chunks, [place[2 * (1 - core) + g] for g in range(groups)], 1), axis=1
    )
    got = other_core(sent)
    first = jnp.where(core == 0, kept, got)
    second = jnp.where(core == 0, got, kept)
    total = jnp.concatenate([first, second], axis=4)
    return jnp.einsum(
        "kgcsr,kct->gsrt", total, inverse, preferred_element_type=jnp.float32
    ).astype(jnp.bfloat16)


def solution(mesh):
    devices = mesh.devices.reshape((2, 2, 4, 4, 2))
    whole = Mesh(devices, ("zl", "core", "x", "y", "zh"))
    pair, shot = ("zl", "core"), ("x", "y", "zh")
    return jax.shard_map(
        local,
        mesh=whole,
        in_specs=(P(pair, shot, None, None), P(shot, None), P()),
        out_specs=P(pair, shot, None, None),
        check_vma=False,
    )
```

time: 427 us -> 252 us (0.59)
  the two profiles are of different devices: /device:TPU:1 before, /device:TPU:83 now
where the time goes in v1:
time: 252 us; the launch traced here: 251 us
  waiting for transfers between devices  136 us (54%)
  local copies, waits for them, and re-layouts  29 us (12%)
  starting transfers between devices  22.6 us (9%)
  between operations  19.1 us (8%)
  Pallas kernels  18.7 us (7%)
  other arithmetic  13.4 us (5%)
  matrix products  12.3 us (5%)
    all_to_all x2, waiting for transfers between devices, local(): chunks = lax.all_to_all(chunks, COLUMN, 0, 0, tiled=True)  124 us
    pallas_call x1, Pallas kernels, chain(): pl.pallas_call(chain_body, grid=(members, shots // rows), in_specs=[pl.Bl...  18.7 us
    all_to_all x2, starting transfers between devices, local(): chunks = lax.all_to_all(chunks, COLUMN, 0, 0, tiled=True)  18.3 us
    ppermute x4, waiting for transfers between devices, other_core(): return lax.ppermute(part, 'core', [(0, 1), (1, 0)])  11.8 us
    dot_general x1, matrix products, local(): jnp.einsum('kct,gsrt->kgcsr', forward, records, preferred_element_type=jn...  7.06 us
    dynamic_slice x3, local copies, waits for them, and re-layouts, pick(): lax.dynamic_index_in_dim(stack, w, axis, keepdims=True)  6.18 us
    dot_general x1, matrix products, local(): jnp.einsum('kgcsr,kct->gsrt', total, inverse, preferred_element_type=jnp....  5.23 us
  transfers between devices with their start and end apart: 6, of which 5 were waited for; matrix products, arithmetic and copies ran while one was open for 2% of the time, Pallas kernels for 0%

profile of v1, /device:TPU:83, one launch (start us, length us, event | category | flops | bytes accessed | tf_op | source)
XLA Modules:
  0.0 251.2 jit_solution(9950932980972016318)
XLA Ops:
  0.2 7.1 %fusion.5 = bf16[32,2,2,24,768]{4,0,3,2,1:T(8,128)(2,1)S(1)} fusion(bf16[2,24,768,128]{3,2,1,0:T(8,128)(2,1)} %param.3, f32[32,1,128]{2,0,1:T(8,128)S(1)} %get-tuple-element.42, f32[32,1,128]{2,0,1:T(8,128)S(1)} %get-tuple-element.41), kind=kOutput, calls=%fused_computation.18 | convolution fusion | flops 606363648 | bytes 14188544 | tf_op jit(solution)/shard_map/kct,gsrt->kgcsr/dot_general | solution.py:121
  7.2 2.1 dynamic-slice_bitcast_fusion
  22.5 3.3 %fusion.9 = (bf16[32,1,2,24,384]{4,0,3,1,2:T(8,128)(2,1)S(1)}, bf16[32,1,2,24,384]{4,0,3,1,2:T(8,128)(2,1)S(1)}, bf16[32,1,2,24,384]{4,0,3,1,2:T(8,128)(2,1)S(1)}, bf16[32,1,2,24,384]{4,0,3,1,2:T(8,128)(2,1)S(1)}) fusion(s32[]{:T(128)S(6)} %select_n.279, bf16[32,2,2,24,384]{4,0,3,1,2:T(8,128)(2,1)S(1)} %get-tuple-element.32, ...), kind=kLoop, calls=%fused_computation.28 | loop fusion | flops 2359296 | bytes 9437200 | tf_op jit(solution)/shard_map/concatenate | solution.py:125
  25.8 0.8 pad_maximum_fusion
  26.6 4.0 %copy.19 = bf16[32,4,2,24,384]{4,3,2,1,0:T(8,128)(2,1)} copy(bf16[32,4,2,24,384]{4,0,3,1,2:T(8,128)(2,1)S(1)} %pad_maximum_fusion) | data formatting | bytes 9437184 | tf_op jit(solution)/shard_map/concatenate | solution.py:129
  30.5 10.0 %all-to-all-start = ((bf16[64,2,2,24,384]{4,3,2,1,0:T(8,128)(2,1)}), bf16[64,2,2,24,384]{4,3,2,1,0:T(8,128)(2,1)}, u32[]{:S(2)}, u32[]{:S(2)}) async-start(bf16[64,2,2,24,384]{4,3,2,1,0:T(8,128)(2,1)} %bitcast.47), calls=%async_computation | async-start | bytes 9437184 | tf_op jit(solution)/shard_map/all_to_all | solution.py:131
  42.0 66.3 %all-to-all-done = bf16[64,2,2,24,384]{4,3,2,1,0:T(8,128)(2,1)} async-done(((bf16[64,2,2,24,384]{4,3,2,1,0:T(8,128)(2,1)}), bf16[64,2,2,24,384]{4,3,2,1,0:T(8,128)(2,1)}, u32[]{:S(2)}, u32[]{:S(2)}) %all-to-all-start) | async-done | bytes 4718624 | tf_op jit(solution)/shard_map/all_to_all | solution.py:131
  108.2 2.8 %constant_dynamic-slice_fusion.12 = (bf16[32,1,2,24,384]{4,3,2,1,0:T(8,128)(2,1)S(1)}, bf16[32,1,2,24,384]{4,3,2,1,0:T(8,128)(2,1)S(1)}, bf16[32,1,2,24,384]{4,3...) fusion(bf16[32,4,2,24,384]{4,3,2,1,0:T(8,128)(2,1)} %bitcast.10, s32[]{:T(128)S(6)} %select_n.296, s32[]{:T(128)S(6)} %select_n.298, ...), kind=kLoop, calls=%fused_computation.65 | loop fusion | bytes 9437200 | tf_op jit(solution)/shard_map/jit(dynamic_index_in_dim)/dynamic_slice | solution.py:96
  111.6 1.7 pad_maximum_fusion.3
  113.3 1.1 collective-permute-start.1
  115.1 3.8 %collective-permute-done.1 = bf16[32,2,2,24,384]{4,0,2,3,1:T(8,128)(2,1)} collective-permute-done((bf16[32,2,2,24,384]{4,0,2,3,1:T(8,128)(2,1)}, bf16[32,2,2,24,384]{4,0,2,3,1:T(8,128)(2,1)}, u32[]{:S(2)}, u32[]{:S(2)}) %collective-permute-start.1) | collective-permute-done | bytes 2359328 | tf_op jit(solution)/shard_map/ppermute | solution.py:100
  118.9 2.1 broadcast_select_fusion.3
  121.7 4.9 %copy.24 = bf16[2,2,32,24,768]{4,3,2,1,0:T(8,128)(2,1)} copy(bf16[2,2,32,24,768]{4,2,1,3,0:T(8,128)(2,1)S(1)} %maximum_bitcast_fusion) | data formatting | bytes 9437184 | tf_op jit(solution)/shard_map/transpose | solution.py:143
  126.6 18.7 %shard_map.37 = bf16[2,2,768,768]{3,2,1,0:T(8,128)(2,1)} custom-call(f32[1,768]{1,0:T(1,128)} %scale_ref.1, bf16[2,2,768,768]{3,2,1,0:T(8,128)(2,1)} %bitcast.43, bf16[2,2,768,768]{3,2,1,0:T(8,128)(2,1)} %bitcast.44), custom_call_target="tpu_custom_call" | custom-call | tf_op jit(solution)/shard_map/pallas_call | solution.py:81
  145.3 4.3 %constant_dynamic-slice_fusion.9 = (bf16[2,2,768,384]{3,2,1,0:T(8,128)(2,1)S(1)}, bf16[2,2,768,384]{3,2,1,0:T(8,128)(2,1)}) fusion(bf16[2,2,768,768]{3,2,1,0:T(8,128)(2,1)} %shard_map.37, s32[]{:T(128)S(6)} %select_n.263, s32[]{:T(128)S(6)} %select_n.264), kind=kLoop, calls=%fused_computation.62 | loop fusion | bytes 9437192 | tf_op jit(solution)/shard_map/dynamic_slice | solution.py:117
  150.0 4.5 %collective-permute-done.2 = bf16[2,2,768,384]{3,2,1,0:T(8,128)(2,1)} collective-permute-done((bf16[2,2,768,384]{3,2,1,0:T(8,128)(2,1)}, bf16[2,2,768,384]{3,2,1,0:T(8,128)(2,1)}, u32[]{:S(2)}, u32[]{:S(2)}) %collective-permute-start.2) | collective-permute-done | bytes 2359328 | tf_op jit(solution)/shard_map/ppermute | solution.py:100
  154.5 2.2 pad_maximum_fusion.1
  158.0 3.0 %copy.48 = bf16[4,2,32,24,384]{4,3,1,0,2:T(8,128)(2,1)} copy(bf16[4,2,32,24,384]{4,3,2,1,0:T(8,128)(2,1)S(1)} %pad_maximum_fusion.2) | data formatting | bytes 9437184 | tf_op jit(solution)/shard_map/concatenate | solution.py:155
  161.0 8.3 %all-to-all-start.1 = ((bf16[64,2,2,24,384]{4,3,2,1,0:T(8,128)(2,1)}), bf16[64,2,2,24,384]{4,3,2,1,0:T(8,128)(2,1)}, u32[]{:S(2)}, u32[]{:S(2)}) async-start(bf16[64,2,2,24,384]{4,3,2,1,0:T(8,128)(2,1)} %bitcast.46), calls=%async_computation.1 | async-start | bytes 9437184 | tf_op jit(solution)/shard_map/all_to_all | solution.py:157
  177.6 58.1 %all-to-all-done.1 = bf16[64,2,2,24,384]{4,3,2,1,0:T(8,128)(2,1)} async-done(((bf16[64,2,2,24,384]{4,3,2,1,0:T(8,128)(2,1)}), bf16[64,2,2,24,384]{4,3,2,1,0:T(8,128)(2,1)}, u32[]{:S(2)}, u32[]{:S(2)}) %all-to-all-start.1) | async-done | bytes 4718624 | tf_op jit(solution)/shard_map/all_to_all | solution.py:157
  235.6 2.8 %constant_dynamic-slice_fusion.2 = (bf16[32,1,2,24,384]{4,3,2,1,0:T(8,128)(2,1)S(1)}, bf16[32,1,2,24,384]{4,3,2,1,0:T(8,128)(2,1)S(1)}, bf16[32,1,2,24,384]{4,3,...) fusion(bf16[32,4,2,24,384]{4,3,2,1,0:T(8,128)(2,1)} %bitcast.19, s32[]{:T(128)S(6)} %select_n.317, s32[]{:T(128)S(6)} %select_n.320, ...), kind=kLoop, calls=%fused_computation.55 | loop fusion | bytes 9437200 | tf_op jit(solution)/shard_map/jit(dynamic_index_in_dim)/dynamic_slice | solution.py:96
  239.3 2.1 collective-permute-start.3
  242.1 3.5 %collective-permute-done.3 = bf16[32,2,2,24,384]{4,0,2,3,1:T(8,128)(2,1)S(1)} collective-permute-done((bf16[32,2,2,24,384]{4,0,2,3,1:T(8,128)(2,1)S(1)}, bf16[32,2,2,24,384]{4,0,2,3,1:T(8,128)(2,1)S(1)}, u32[]{:S(2)}, u32[]{:S(2)}) %collective-permute-start.3) | collective-permute-done | bytes 2359328 | tf_op jit(solution)/shard_map/ppermute | solution.py:100
  246.0 5.2 %bitcast_convert_fusion = bf16[2,24,768,128]{3,2,1,0:T(8,128)(2,1)} fusion(bf16[32,2,2,24,384]{4,0,2,3,1:T(8,128)(2,1)S(1)} %get-tuple-element.10, bf16[32,2,2,24,384]{4,0,2,3,1:T(8,128)(2,1)S(1)} %get-tuple-element.9, f32[32,1,128]{2,0,1:T(8,128)S(1)} %get-tuple-element.42, f32[32,1,128]{2,0,1:T(8,128)S(1)} %get-tuple-element.41), kind=kOutput, calls=%fused_computation | convolution fusion | flops 618160128 | bytes 14188544 | tf_op jit(solution)/shard_map/kgcsr,kct->gsrt/dot_general | solution.py:167
  (31 shorter events, 9.5 us)
Async XLA Ops:
  7.2 2.8 %copy-start = (s32[8]{0:T(128)S(1)}, s32[8]{0:T(128)}, u32[]{:S(2)}) copy-start(s32[8]{0:T(128)} %param.5) | copy-start | bytes 100
  9.4 13.1 %collective-permute-start = (bf16[32,2,2,24,384]{4,0,3,1,2:T(8,128)(2,1)}, bf16[32,2,2,24,384]{4,0,3,1,2:T(8,128)(2,1)}, u32[]{:S(2)}, u32[]{:S(2)}) collective-permute-start(bf16[32,2,2,24,384]{4,0,3,1,2:T(8,128)(2,1)} %get-tuple-element.31), channel_id=1, source_target_pairs={{0,32},{32,0},{1,33},{33,1},{2,34},{34,2},{3,35},{35,3},{4,36},{36... | collective-permute-start | bytes 7077896 | tf_op jit(solution)/shard_map/ppermute | solution.py:100
  30.5 77.7 %all-to-all-start = ((bf16[64,2,2,24,384]{4,3,2,1,0:T(8,128)(2,1)}), bf16[64,2,2,24,384]{4,3,2,1,0:T(8,128)(2,1)}, u32[]{:S(2)}, u32[]{:S(2)}) async-start(bf16[64,2,2,24,384]{4,3,2,1,0:T(8,128)(2,1)} %bitcast.47), calls=%async_computation | async-start | bytes 9437184 | tf_op jit(solution)/shard_map/all_to_all | solution.py:131
  113.3 5.6 %collective-permute-start.1 = (bf16[32,2,2,24,384]{4,0,2,3,1:T(8,128)(2,1)}, bf16[32,2,2,24,384]{4,0,2,3,1:T(8,128)(2,1)}, u32[]{:S(2)}, u32[]{:S(2)}) collective-permute-start(bf16[32,2,2,24,384]{4,0,2,3,1:T(8,128)(2,1)} %pad_maximum_fusion.3), channel_id=1, source_target_pairs={{0,32},{32,0},{1,33},{33,1},{2,34},{34,2},{3,35},{35,3},{4,36},{36... | collective-permute-start | bytes 7077896 | tf_op jit(solution)/shard_map/ppermute | solution.py:100
  149.6 4.9 %collective-permute-start.2 = (bf16[2,2,768,384]{3,2,1,0:T(8,128)(2,1)}, bf16[2,2,768,384]{3,2,1,0:T(8,128)(2,1)}, u32[]{:S(2)}, u32[]{:S(2)}) collective-permute-start(bf16[2,2,768,384]{3,2,1,0:T(8,128)(2,1)} %get-tuple-element.20), channel_id=1, source_target_pairs={{0,32},{32,0},{1,33},{33,1},{2,34},{34,2},{3,35},{35,3},{4,36},{36... | collective-permute-start | bytes 7077896 | tf_op jit(solution)/shard_map/ppermute | solution.py:100
  161.0 74.6 %all-to-all-start.1 = ((bf16[64,2,2,24,384]{4,3,2,1,0:T(8,128)(2,1)}), bf16[64,2,2,24,384]{4,3,2,1,0:T(8,128)(2,1)}, u32[]{:S(2)}, u32[]{:S(2)}) async-start(bf16[64,2,2,24,384]{4,3,2,1,0:T(8,128)(2,1)} %bitcast.46), calls=%async_computation.1 | async-start | bytes 9437184 | tf_op jit(solution)/shard_map/all_to_all | solution.py:157
  239.3 6.3 %collective-permute-start.3 = (bf16[32,2,2,24,384]{4,0,2,3,1:T(8,128)(2,1)S(1)}, bf16[32,2,2,24,384]{4,0,2,3,1:T(8,128)(2,1)S(1)}, u32[]{:S(2)}, u32[]{:S(2)}) collective-permute-start(bf16[32,2,2,24,384]{4,0,2,3,1:T(8,128)(2,1)S(1)} %pad_maximum_fusion.4), channel_id=1, source_target_pairs={{0,32},{32,0},{1,33},{33,1},{2,34},{34,2},{3,35},{35,3},{4,36},{36... | collective-permute-start | bytes 7077896 | tf_op jit(solution)/shard_map/ppermute | solution.py:100

commit v2 on v0

v2 whole, which is shorter than its diff:
```python
import math

import jax
import jax.numpy as jnp
from jax import lax
from jax.experimental import pallas as pl
from jax.experimental.pallas import tpu as pltpu
from jax.sharding import Mesh
from jax.sharding import PartitionSpec as P

COLUMN = ("x", "y", "zh", "zl")
ROWS = 384
SUBLANES = 8
GROUPS = 8
VMEM_LIMIT = 56 << 20


def make_tables(freqs, time):
    product = (
        jnp.arange(1, freqs + 1, dtype=jnp.int32)[:, None]
        * jnp.arange(time, dtype=jnp.int32)[None, :]
        % time
    )
    phase = product.astype(jnp.float32) * (2.0 * math.pi / time)
    cosine = jnp.cos(phase)
    sine = jnp.sin(phase)
    forward = (jnp.stack([cosine, -sine], axis=1) * math.sqrt(2.0 / time)).astype(jnp.bfloat16)
    inverse = (jnp.stack([cosine, -sine], axis=1) / math.sqrt(freqs)).astype(jnp.bfloat16)
    return (forward, inverse)


OWN_SLOT = 0
OTHER_SLOT = 2
OWN_MEMBER = 4
OTHER_MEMBER = 6
HALF = 8
OTHER_HALF = 9
FLAT = 10
ENTRIES = 12


def deal_body(mirror_ref, here_ref, table_ref):
    half = GROUPS // 2
    chip, core = here_ref[0], here_ref[1]
    mirror = [mirror_ref[g] for g in range(GROUPS)]
    zero, one = jnp.int32(0), jnp.int32(1)

    def flag(condition):
        return jnp.where(condition, one, zero)

    upper = [flag(m >= half) for m in mirror]
    within = [upper[g] if g >= half else 1 - upper[g] for g in range(GROUPS)]
    crossing = GROUPS - sum(within[1:], within[0])
    low = [jnp.minimum(m, g) for g, m in enumerate(mirror)]
    color, key = [], []
    for g in range(GROUPS):
        with_first = flag(mirror[g] - half * upper[g] == 0) if g % half else one
        color.append(
            jnp.where(
                crossing == GROUPS,
                flag(low[g] >= half // 2),
                jnp.where(crossing == half, 1 - within[g], 1 - with_first),
            )
        )
        key.append(jnp.where(within[g] == 1, g, low[g]))
    place = []
    for g in range(GROUPS):
        rank = zero
        for other in range(g // half * half, g // half * half + half):
            if other != g:
                rank = rank + flag(color[g] == color[other]) * flag(key[other] < key[g])
        place.append(2 * color[g] + rank)
    mine = [jnp.where(chip == 0, place[g], place[half + g]) for g in range(half)]
    for g in range(2):
        table_ref[OWN_SLOT + g] = jnp.where(core == 0, mine[g], mine[2 + g])
        table_ref[OTHER_SLOT + g] = jnp.where(core == 0, mine[2 + g], mine[g])
    mixed = jnp.where(chip == 0, flag(crossing == GROUPS), flag(crossing >= half))
    for j in range(2):
        table_ref[OWN_MEMBER + j] = jnp.where(mixed == 1, 2 * j + core, 2 * core + j)
        table_ref[OTHER_MEMBER + j] = jnp.where(mixed == 1, 2 * j + 1 - core, 2 * (1 - core) + j)
    table_ref[HALF] = core
    table_ref[OTHER_HALF] = 1 - core
    table_ref[FLAT] = zero
    table_ref[FLAT + 1] = one


def deal(mirror, here):
    smem = pl.BlockSpec(memory_space=pltpu.SMEM)
    return pl.pallas_call(
        deal_body,
        in_specs=[smem, smem],
        out_specs=smem,
        out_shape=jax.ShapeDtypeStruct((ENTRIES,), jnp.int32),
        name="deal",
    )(mirror, here)


def params():
    return pltpu.CompilerParams(vmem_limit_bytes=VMEM_LIMIT)


def two_shots(taps_ref):
    taps = taps_ref[...]
    blank = jnp.zeros_like(taps)
    return jnp.concatenate(
        [jnp.concatenate([taps, blank], axis=1), jnp.concatenate([blank, taps], axis=1)], axis=0
    )


def forward_transform(table, forward, records, half, slots, count):
    groups, shots, recv, time = records.shape
    parts = forward.shape[0]
    width = recv // 2
    tiles = shots // SUBLANES

    def body(table_ref, forward_ref, records_ref, out_ref, held, spectra, in_sems, out_sems):
        start = pl.multiple_of(table_ref[half] * width, width)
        ins, outs = [], []
        for i in range(groups * tiles):
            g, s = divmod(i, tiles)
            source = records_ref.at[g, pl.ds(s * SUBLANES, SUBLANES), pl.ds(start, width)]
            ins.append(pltpu.make_async_copy(source, held.at[i], in_sems.at[i]))
        for copy in ins:
            copy.start()
        two = two_shots(forward_ref)
        for i in range(groups * tiles):
            g, s = divmod(i, tiles)
            ins[i].wait()
            found = []
            for q in range(0, SUBLANES, 2):
                both = jnp.concatenate([held[i, q], held[i, q + 1]], axis=1)
                found.append(
                    lax.dot_general(
                        two, both, (((1,), (1,)), ((), ())), preferred_element_type=jnp.float32
                    )
                )
            found = jnp.concatenate(found, axis=0).reshape((SUBLANES, parts, width))
            found = jnp.transpose(found, (1, 0, 2)).reshape((parts // 2, 2, SUBLANES, width))
            spectra[g, :, :, s * SUBLANES : (s + 1) * SUBLANES, :] = found.astype(jnp.bfloat16)
            if s == tiles - 1:
                target = out_ref.at[:, table_ref[slots + g]]
                outs.append(pltpu.make_async_copy(spectra.at[g], target, out_sems.at[g]))
                outs[-1].start()
        for copy in outs:
            copy.wait()

    return pl.pallas_call(
        body,
        in_specs=[
            pl.BlockSpec(memory_space=pltpu.SMEM),
            pl.BlockSpec(memory_space=pltpu.VMEM),
            pl.BlockSpec(memory_space=pl.ANY),
        ],
        out_specs=pl.BlockSpec(memory_space=pl.ANY),
        out_shape=jax.ShapeDtypeStruct((parts // 2, count, 2, shots, width), jnp.bfloat16),
        scratch_shapes=[
            pltpu.VMEM((groups * tiles, SUBLANES, width, time), jnp.bfloat16),
            pltpu.VMEM((groups, parts // 2, 2, shots, width), jnp.bfloat16),
            pltpu.SemaphoreType.DMA((groups * tiles,)),
            pltpu.SemaphoreType.DMA((groups,)),
        ],
        compiler_params=params(),
        name="forward",
    )(table, forward, records)


def copy_slots(pairs, sems):
    copies = [pltpu.make_async_copy(a, b, sems.at[i]) for i, (a, b) in enumerate(pairs)]
    for copy in copies:
        copy.start()
    for copy in copies:
        copy.wait()


def gather(table, whole, slots):
    blocks, _, parts, shots, width = whole.shape

    def body(table_ref, whole_ref, part_ref, sems):
        copy_slots(
            [(whole_ref.at[:, table_ref[slots + j]], part_ref.at[:, j]) for j in range(2)], sems
        )

    return pl.pallas_call(
        body,
        in_specs=[pl.BlockSpec(memory_space=pltpu.SMEM), pl.BlockSpec(memory_space=pl.ANY)],
        out_specs=pl.BlockSpec(memory_space=pltpu.VMEM),
        out_shape=jax.ShapeDtypeStruct((blocks, 2, parts, shots, width), jnp.bfloat16),
        scratch_shapes=[pltpu.SemaphoreType.DMA((2,))],
        compiler_params=params(),
        name="gather",
    )(table, whole)


def scatter(table, part, whole, slots):
    def body(table_ref, part_ref, whole_ref, out_ref, sems):
        copy_slots(
            [(part_ref.at[:, j], out_ref.at[:, table_ref[slots + j]]) for j in range(2)], sems
        )

    return pl.pallas_call(
        body,
        in_specs=[
            pl.BlockSpec(memory_space=pltpu.SMEM),
            pl.BlockSpec(memory_space=pltpu.VMEM),
            pl.BlockSpec(memory_space=pl.ANY),
        ],
        out_specs=pl.BlockSpec(memory_space=pl.ANY),
        out_shape=jax.ShapeDtypeStruct(whole.shape, jnp.bfloat16),
        scratch_shapes=[pltpu.SemaphoreType.DMA((2,))],
        input_output_aliases={2: 0},
        compiler_params=params(),
        name="scatter",
    )(table, part, whole)


def chain_body(
    table_ref, scale_ref, kept_0_ref, kept_1_ref, got_ref, own_ref, other_ref, spectra_ref
):
    member, tile = pl.program_id(0), pl.program_id(1)
    blocks, _, _, shots, width = got_ref.shape
    size = blocks * shots
    core = table_ref[HALF]

    @pl.when((member == 0) & (tile == 0))
    def _():
        for value in range(2):

            @pl.when(core == value)
            def _():
                for j, kept_ref in enumerate((kept_0_ref, kept_1_ref)):
                    for c in range(2):
                        kept = kept_ref[:, 0, c].reshape((size, width))
                        got = got_ref[:, j, c].reshape((size, width))
                        spectra_ref[j, c, :, value * width : (value + 1) * width] = kept
                        spectra_ref[j, c, :, (1 - value) * width : (2 - value) * width] = got

    rows = own_ref.shape[0] * shots
    scale = -scale_ref[...] / math.sqrt(2.0 * scale_ref.shape[-1])
    mate_re = spectra_ref[1 - member, 0]
    mate_im = spectra_ref[1 - member, 1]

    def dot(a, b):
        return jnp.dot(a, b, preferred_element_type=jnp.float32)

    def times(left_re, left_im):
        real = dot(left_re, mate_re) - dot(left_im, mate_im)
        imag = dot(left_re, mate_im) + dot(left_im, mate_re)
        return real, imag

    def scaled(part):
        return (part * scale).astype(jnp.bfloat16)

    window = pl.ds(pl.multiple_of(tile * rows, rows), rows)
    real_1, imag_1 = times(
        scaled(spectra_ref[member, 0, window, :].astype(jnp.float32)),
        scaled(spectra_ref[member, 1, window, :].astype(jnp.float32)),
    )
    real_2, imag_2 = times(scaled(real_1), scaled(imag_1))
    for c, total in enumerate((real_1 + real_2, imag_1 + imag_2)):
        total = total.astype(jnp.bfloat16)
        low = total[:, :width].reshape((rows // shots, shots, width))
        high = total[:, width:].reshape((rows // shots, shots, width))

        @pl.when(core == 0)
        def _():
            own_ref[:, 0, c] = low
            other_ref[:, 0, c] = high

        @pl.when(core == 1)
        def _():
            own_ref[:, 0, c] = high
            other_ref[:, 0, c] = low


def chain(table, surface, kept, got):
    blocks, count, parts, shots, width = kept.shape
    tile = ROWS // shots
    tiles = blocks // tile
    whole = (blocks, 1, parts, shots, width)
    part = (tile, 1, parts, shots, width)
    return pl.pallas_call(
        chain_body,
        grid_spec=pltpu.PrefetchScalarGridSpec(
            num_scalar_prefetch=1,
            grid=(2, tiles),
            in_specs=[
                pl.BlockSpec((1, 2 * width), lambda j, m, t: (0, 0)),
                pl.BlockSpec(whole, lambda j, m, t: (0, t[OWN_MEMBER], 0, 0, 0)),
                pl.BlockSpec(whole, lambda j, m, t: (0, t[OWN_MEMBER + 1], 0, 0, 0)),
                pl.BlockSpec(memory_space=pltpu.VMEM),
            ],
            out_specs=[
                pl.BlockSpec(part, lambda j, m, t: (m, t[OWN_MEMBER + j], 0, 0, 0)),
                pl.BlockSpec(part, lambda j, m, t: (m, j, 0, 0, 0)),
            ],
            scratch_shapes=[pltpu.VMEM((2, parts, blocks * shots, 2 * width), jnp.bfloat16)],
        ),
        out_shape=[
            jax.ShapeDtypeStruct(kept.shape, jnp.bfloat16),
            jax.ShapeDtypeStruct(got.shape, jnp.bfloat16),
        ],
        compiler_params=params(),
        name="chain",
    )(table, surface, kept, kept, got)


def inverse_transform(table, inverse, total, half, slots, whole=None):
    freqs, count, parts, shots, width = total.shape
    rows, time = inverse.shape
    tiles = shots // SUBLANES
    groups = 2
    pieces = 2
    local_input = count == groups

    def body(table_ref, inverse_ref, total_ref, *refs):
        out_ref, held, predicted, in_sems, out_sems = refs[-5:]
        start = pl.multiple_of(table_ref[half] * width, width)
        ins, outs = [], []
        if not local_input:
            for g in range(groups):
                for p in range(pieces):
                    some = pl.ds(p * freqs // pieces, freqs // pieces)
                    source = total_ref.at[some, table_ref[slots + g]]
                    ins.append(
                        pltpu.make_async_copy(source, held.at[g, some], in_sems.at[g, p])
                    )
            for copy in ins:
                copy.start()
        two = two_shots(inverse_ref)
        for g in range(groups):
            if not local_input:
                for copy in ins[g * pieces : (g + 1) * pieces]:
                    copy.wait()
            for s in range(tiles):
                window = slice(s * SUBLANES, (s + 1) * SUBLANES)
                block = total_ref[:, g, :, window, :] if local_input else held[g, :, :, window, :]
                block = block.astype(jnp.float32).reshape((rows, SUBLANES, width))
                block = jnp.transpose(block, (1, 0, 2)).astype(jnp.bfloat16)
                i = g * tiles + s
                for q in range(0, SUBLANES, 2):
                    both = jnp.concatenate([block[q], block[q + 1]], axis=0)
                    traces = lax.dot_general(
                        both, two, (((0,), (0,)), ((), ())), preferred_element_type=jnp.float32
                    ).astype(jnp.bfloat16)
                    predicted[i, q] = traces[:, :time]
                    predicted[i, q + 1] = traces[:, time:]
                target = out_ref.at[g, pl.ds(s * SUBLANES, SUBLANES), pl.ds(start, width)]
                outs.append(pltpu.make_async_copy(predicted.at[i], target, out_sems.at[i]))
                outs[-1].start()
        for copy in outs:
            copy.wait()

    specs = [
        pl.BlockSpec(memory_space=pltpu.SMEM),
        pl.BlockSpec(memory_space=pltpu.VMEM),
        pl.BlockSpec(memory_space=pltpu.VMEM if local_input else pl.ANY),
    ]
    operands = [table, inverse, total]
    aliases = {}
    if whole is not None:
        specs.append(pl.BlockSpec(memory_space=pl.ANY))
        operands.append(whole)
        aliases = {3: 0}
    return pl.pallas_call(
        body,
        in_specs=specs,
        out_specs=pl.BlockSpec(memory_space=pl.ANY),
        out_shape=jax.ShapeDtypeStruct((groups, shots, 2 * width, time), jnp.bfloat16),
        scratch_shapes=[
            pltpu.VMEM((groups, freqs, parts, shots, width), jnp.bfloat16),
            pltpu.VMEM((groups * tiles, SUBLANES, width, time), jnp.bfloat16),
            pltpu.SemaphoreType.DMA((groups, pieces)),
            pltpu.SemaphoreType.DMA((groups * tiles,)),
        ],
        input_output_aliases=aliases,
        compiler_params=params(),
        name="inverse",
    )(*operands)


def other_core(part):
    part = lax.ppermute(part, "core", [(0, 1), (1, 0)])
    return pltpu.with_memory_space_constraint(part, pltpu.VMEM)


def exchange(chunks):
    blocks, count, parts, shots, width = chunks.shape
    chunks = chunks.reshape((2 * blocks, count // 2, parts, shots, width))
    chunks = lax.all_to_all(chunks, COLUMN, 0, 0, tiled=True)
    return chunks.reshape((blocks, count, parts, shots, width))


def local(records, surface, mirror):
    freqs = lax.axis_size("x") * lax.axis_size("y") * lax.axis_size("zh")
    time = records.shape[-1]
    forward, inverse = make_tables(freqs, time)
    forward = forward.reshape((2 * freqs, time))
    inverse = inverse.reshape((2 * freqs, time))
    here = jnp.stack([lax.axis_index("zl"), lax.axis_index("core")]).astype(jnp.int32)
    table = deal(mirror, here)

    sent = forward_transform(table, forward, records, OTHER_HALF, FLAT, 2)
    chunks = forward_transform(table, forward, records, HALF, OWN_SLOT, 4)
    chunks = scatter(table, other_core(sent), chunks, OTHER_SLOT)
    chunks = exchange(chunks)
    got = other_core(gather(table, chunks, OTHER_MEMBER))
    own, other = chain(table, surface, chunks, got)
    chunks = scatter(table, other_core(other), own, OTHER_MEMBER)
    chunks = exchange(chunks)
    got = other_core(gather(table, chunks, OTHER_SLOT))
    predicted = inverse_transform(table, inverse, chunks, HALF, OWN_SLOT)
    return inverse_transform(table, inverse, got, OTHER_HALF, FLAT, predicted)


def solution(mesh):
    devices = mesh.devices.reshape((2, 2, 4, 4, 2))
    whole = Mesh(devices, ("zl", "core", "x", "y", "zh"))
    pair, shot = ("zl", "core"), ("x", "y", "zh")
    return jax.shard_map(
        local,
        mesh=whole,
        in_specs=(P(pair, shot, None, None), P(shot, None), P()),
        out_specs=P(pair, shot, None, None),
        check_vma=False,
    )
```

time: 427 us -> 201 us (0.47)
  waiting for transfers between devices: 163 us -> 8.75 us
  matrix products: 64.6 us -> 0 us
  Pallas kernels: 0 us -> 52.5 us
  local copies, waits for them, and re-layouts: 37.6 us -> 1.23 us
  between operations: 13.5 us -> 0.26 us
  other arithmetic: 13 us -> 0.75 us
  starting transfers between devices: 0.01 us -> 5.72 us
    all_gather x1 -> x0, waiting for transfers between devices: 163 us -> none  [local(): piece = lax.all_gather(own_spec, 'pair', axis=0, tiled=True)]
    dot_general x11 -> x0, matrix products: 64.6 us -> none  [the longest x8 38.5 us: batch_dot(): jnp.einsum('kij,kjl->kil', left, right, preferred_element_type=jnp.float32)]
    pallas_call x0 -> x10, Pallas kernels: none -> 52.5 us  [the longest x1 19.9 us: chain(): pl.pallas_call(chain_body, grid_spec=pltpu.PrefetchScalarGridSpec(num_sca...]
    unnamed x12 -> x0, local copies, waits for them, and re-layouts: 23.1 us -> none
    convert_element_type x3 -> x1, other arithmetic: 12.9 us -> 0.01 us  [make_tables(): (jnp.stack([cosine, -sine], axis=1) * math.sqrt(2.0 / time)).astype(jnp.b...]
    convert_element_type x2, local copies, waits for them, and re-layouts: 11.9 us -> 1.23 us  [the longest x1 0.62 us: make_tables(): (jnp.stack([cosine, -sine], axis=1) / math.sqrt(freqs)).astype(jnp.bfloat16)]
    ppermute x0 -> x4, waiting for transfers between devices: none -> 8.75 us  [other_core(): part = lax.ppermute(part, 'core', [(0, 1), (1, 0)])]
    ppermute x0 -> x4, starting transfers between devices: none -> 5.72 us  [other_core(): part = lax.ppermute(part, 'core', [(0, 1), (1, 0)])]
  transfers between devices with their start and end apart: 1 -> 4, of which waited for: 1 -> 2; matrix products, arithmetic and copies ran while one was open for 1% -> 0% of each run, Pallas kernels for 0% -> 5%
where the time goes in v2:
time: 201 us
  blocking collectives  131 us (65%)
  Pallas kernels  52.5 us (26%)
  waiting for transfers between devices  8.75 us (4%)
  starting transfers between devices  5.72 us (3%)
    all_to_all x2, blocking collectives, exchange(): chunks = lax.all_to_all(chunks, COLUMN, 0, 0, tiled=True)  131 us
    pallas_call x1, Pallas kernels, chain(): pl.pallas_call(chain_body, grid_spec=pltpu.PrefetchScalarGridSpec(num_sca...  19.9 us
    pallas_call x2, Pallas kernels, forward_transform(): pl.pallas_call(body, in_specs=[pl.BlockSpec(memory_space=pltpu.SMEM), pl....  11.4 us
    ppermute x4, waiting for transfers between devices, other_core(): part = lax.ppermute(part, 'core', [(0, 1), (1, 0)])  8.75 us
    pallas_call x2, Pallas kernels, inverse_transform(): pl.pallas_call(body, in_specs=specs, out_specs=pl.BlockSpec(memory_space=...  8.3 us
    pallas_call x2, Pallas kernels, gather(): pl.pallas_call(body, in_specs=[pl.BlockSpec(memory_space=pltpu.SMEM), pl....  7.45 us
    ppermute x4, starting transfers between devices, other_core(): part = lax.ppermute(part, 'core', [(0, 1), (1, 0)])  5.72 us
    pallas_call x2, Pallas kernels, scatter(): pl.pallas_call(body, in_specs=[pl.BlockSpec(memory_space=pltpu.SMEM), pl....  4.17 us
  transfers between devices with their start and end apart: 4, of which 2 were waited for; matrix products, arithmetic and copies ran while one was open for 0% of the time, Pallas kernels for 5%

profile of v2, /device:TPU:1, one launch (start us, length us, event | category | flops | bytes accessed | tf_op | source)
XLA Modules:
  0.0 200.6 jit_solution(17958663392985243979)
XLA Ops:
  0.0 0.2 fusion.6
  0.2 0.6 copy.8
  0.8 0.6 pad_add_fusion.here_ref
  1.4 1.3 deal.1.table_ref
  2.7 5.7 %forward.2 = bf16[32,2,2,24,384]{4,3,2,1,0:T(8,128)(2,1)} custom-call(s32[12]{0:T(128)} %deal.1.table_ref, bf16[64,128]{1,0:T(8,128)(2,1)} %bitcast.15, bf16[2,24,768,128]{3,2,1,0:T(8,128)(2,1)} %records_ref.3), custom_call_target="tpu_custom_call" | custom-call | tf_op jit(solution)/shard_map/forward/pallas_call | solution.py:147
  8.4 1.5 collective-permute-start
  9.9 5.7 %forward.3.whole_ref = bf16[32,4,2,24,384]{4,3,2,1,0:T(8,128)(2,1)} custom-call(s32[12]{0:T(128)} %deal.1.table_ref, bf16[64,128]{1,0:T(8,128)(2,1)} %bitcast.16, bf16[2,24,768,128]{3,2,1,0:T(8,128)(2,1)} %records_ref.3), custom_call_target="tpu_custom_call" | custom-call | tf_op jit(solution)/shard_map/forward/pallas_call | solution.py:147
  15.6 0.0 collective-permute-done.part_ref
  15.6 2.1 %scatter.2 = bf16[32,4,2,24,384]{4,3,2,1,0:T(8,128)(2,1)} custom-call(s32[12]{0:T(128)} %deal.1.table_ref, bf16[32,2,2,24,384]{4,3,2,1,0:T(8,128)(2,1)S(1)} %collective-permute-done.part_ref, bf16[32,4,2,24,384]{4,3,2,1,0:T(8,128)(2,1)} %forward.3.whole_ref), custom_call_target="tpu_custom_call", output_to_operand_aliasing={{}: (2, {})} | custom-call | tf_op jit(solution)/shard_map/scatter/pallas_call | solution.py:200
  17.7 68.6 %all_to_all.10 = bf16[64,2,2,24,384]{4,3,2,1,0:T(8,128)(2,1)} all-to-all(bf16[64,2,2,24,384]{4,3,2,1,0:T(8,128)(2,1)} %bitcast.13), channel_id=1, replica_groups=mesh['zl'=2,'core'=2,'x'=4,'y'=4,'zh'=2] {'x','y','zh','zl'}, dimensions={0} | all-to-all | bytes 9437184 | tf_op jit(solution)/shard_map/all_to_all | solution.py:389
  86.4 3.7 %gather.2 = bf16[32,2,2,24,384]{4,3,2,1,0:T(8,128)(2,1)} custom-call(s32[12]{0:T(128)} %deal.1.table_ref, bf16[32,4,2,24,384]{4,3,2,1,0:T(8,128)(2,1)} %bitcast.8), custom_call_target="tpu_custom_call" | custom-call | tf_op jit(solution)/shard_map/gather/pallas_call | solution.py:183
  90.1 1.7 collective-permute-start.1
  91.8 4.4 %collective-permute-done.1.got_ref = bf16[32,2,2,24,384]{4,3,2,1,0:T(8,128)(2,1)S(1)} collective-permute-done((bf16[32,2,2,24,384]{4,3,2,1,0:T(8,128)(2,1)}, bf16[32,2,2,24,384]{4,3,2,1,0:T(8,128)(2,1)S(1)}, u32[]{:S(2)}, u32[]{:S(2)}) %collective-permute-start.1) | collective-permute-done | bytes 2359328 | tf_op jit(solution)/shard_map/ppermute | solution.py:382
  96.2 19.9 %chain.1 = (bf16[32,4,2,24,384]{4,3,2,1,0:T(8,128)(2,1)}, bf16[32,2,2,24,384]{4,3,2,1,0:T(8,128)(2,1)}) custom-call(s32[12]{0:T(128)} %deal.1.table_ref, f32[1,768]{1,0:T(1,128)} %scale_ref.1, bf16[32,4,2,24,384]{4,3,2,1,0:T(8,128)(2,1)} %bitcast.9, bf16[32,4,2,24,384]{4,3,2,1,0:T(8,128)(2,1)} %bitcast.10, ...), custom_call_target="tpu_custom_call" | custom-call | tf_op jit(solution)/shard_map/chain/pallas_call | solution.py:281
  116.0 0.4 collective-permute-start.2
  116.4 4.4 %collective-permute-done.2.part_ref = bf16[32,2,2,24,384]{4,3,2,1,0:T(8,128)(2,1)S(1)} collective-permute-done((bf16[32,2,2,24,384]{4,3,2,1,0:T(8,128)(2,1)}, bf16[32,2,2,24,384]{4,3,2,1,0:T(8,128)(2,1)S(1)}, u32[]{:S(2)}, u32[]{:S(2)}) %collective-permute-start.2) | collective-permute-done | bytes 2359328 | tf_op jit(solution)/shard_map/ppermute | solution.py:382
  120.8 2.1 %scatter.3 = bf16[32,4,2,24,384]{4,3,2,1,0:T(8,128)(2,1)} custom-call(s32[12]{0:T(128)} %deal.1.table_ref, bf16[32,2,2,24,384]{4,3,2,1,0:T(8,128)(2,1)S(1)} %collective-permute-done.2.part_ref, bf16[32,4,2,24,384]{4,3,2,1,0:T(8,128)(2,1)} %get-tuple-element.8.whole_ref), custom_call_target="tpu_custom_call", output_to_operand_aliasing={{}: (2, {})} | custom-call | tf_op jit(solution)/shard_map/scatter/pallas_call | solution.py:200
  122.9 62.8 %all_to_all.11 = bf16[64,2,2,24,384]{4,3,2,1,0:T(8,128)(2,1)} all-to-all(bf16[64,2,2,24,384]{4,3,2,1,0:T(8,128)(2,1)} %bitcast.14), channel_id=1, replica_groups=mesh['zl'=2,'core'=2,'x'=4,'y'=4,'zh'=2] {'x','y','zh','zl'}, dimensions={0} | all-to-all | bytes 9437184 | tf_op jit(solution)/shard_map/all_to_all | solution.py:389
  185.6 3.7 %gather.3 = bf16[32,2,2,24,384]{4,3,2,1,0:T(8,128)(2,1)} custom-call(s32[12]{0:T(128)} %deal.1.table_ref, bf16[32,4,2,24,384]{4,3,2,1,0:T(8,128)(2,1)} %bitcast.11), custom_call_target="tpu_custom_call" | custom-call | tf_op jit(solution)/shard_map/gather/pallas_call | solution.py:183
  189.4 2.1 %collective-permute-start.3 = (bf16[32,2,2,24,384]{4,3,2,1,0:T(8,128)(2,1)}, bf16[32,2,2,24,384]{4,3,2,1,0:T(8,128)(2,1)S(1)}, u32[]{:S(2)}, u32[]{:S(2)}) collective-permute-start(bf16[32,2,2,24,384]{4,3,2,1,0:T(8,128)(2,1)} %gather.3), channel_id=1, source_target_pairs={{0,32},{32,0},{1,33},{33,1},{2,34},{34,2},{3,35},{35,3},{4,36},{36... | collective-permute-start | bytes 7077896 | tf_op jit(solution)/shard_map/ppermute | solution.py:382
  191.5 0.6 copy.7
  192.1 4.8 %inverse.2.refs_0_ = bf16[2,24,768,128]{3,2,1,0:T(8,128)(2,1)} custom-call(s32[12]{0:T(128)} %deal.1.table_ref, bf16[64,128]{1,0:T(8,128)(2,1)} %bitcast.17, bf16[32,4,2,24,384]{4,3,2,1,0:T(8,128)(2,1)} %bitcast.12), custom_call_target="tpu_custom_call" | custom-call | tf_op jit(solution)/shard_map/inverse/pallas_call | solution.py:364
  196.9 0.0 collective-permute-done.3.total_ref
  196.9 3.5 %inverse.3 = bf16[2,24,768,128]{3,2,1,0:T(8,128)(2,1)} custom-call(s32[12]{0:T(128)} %deal.1.table_ref, bf16[64,128]{1,0:T(8,128)(2,1)} %bitcast.18, bf16[32,2,2,24,384]{4,3,2,1,0:T(8,128)(2,1)S(1)} %collective-permute-done.3.total_ref, bf16[2,24,768,128]{3,2,1,0:T(8,128)(2,1)} %inverse.2.refs_0_), custom_call_target="tpu_custom_call", output_to_operand_aliasing={{}: (3, {})} | custom-call | tf_op jit(solution)/shard_map/inverse/pallas_call | solution.py:364
  (2 shorter events, 0.0 us)
Async XLA Ops:
  8.4 7.2 %collective-permute-start = (bf16[32,2,2,24,384]{4,3,2,1,0:T(8,128)(2,1)}, bf16[32,2,2,24,384]{4,3,2,1,0:T(8,128)(2,1)S(1)}, u32[]{:S(2)}, u32[]{:S(2)}) collective-permute-start(bf16[32,2,2,24,384]{4,3,2,1,0:T(8,128)(2,1)} %forward.2), channel_id=1, source_target_pairs={{0,32},{32,0},{1,33},{33,1},{2,34},{34,2},{3,35},{35,3},{4,36},{36... | collective-permute-start | bytes 7077896 | tf_op jit(solution)/shard_map/ppermute | solution.py:382
  90.1 6.1 %collective-permute-start.1 = (bf16[32,2,2,24,384]{4,3,2,1,0:T(8,128)(2,1)}, bf16[32,2,2,24,384]{4,3,2,1,0:T(8,128)(2,1)S(1)}, u32[]{:S(2)}, u32[]{:S(2)}) collective-permute-start(bf16[32,2,2,24,384]{4,3,2,1,0:T(8,128)(2,1)} %gather.2), channel_id=1, source_target_pairs={{0,32},{32,0},{1,33},{33,1},{2,34},{34,2},{3,35},{35,3},{4,36},{36... | collective-permute-start | bytes 7077896 | tf_op jit(solution)/shard_map/ppermute | solution.py:382
  116.0 4.8 %collective-permute-start.2 = (bf16[32,2,2,24,384]{4,3,2,1,0:T(8,128)(2,1)}, bf16[32,2,2,24,384]{4,3,2,1,0:T(8,128)(2,1)S(1)}, u32[]{:S(2)}, u32[]{:S(2)}) collective-permute-start(bf16[32,2,2,24,384]{4,3,2,1,0:T(8,128)(2,1)} %get-tuple-element.7), channel_id=1, source_target_pairs={{0,32},{32,0},{1,33},{33,1},{2,34},{34,2},{3,35},{35,3},{4,36},{36... | collective-permute-start | bytes 7077896 | tf_op jit(solution)/shard_map/ppermute | solution.py:382
  189.4 7.6 %collective-permute-start.3 = (bf16[32,2,2,24,384]{4,3,2,1,0:T(8,128)(2,1)}, bf16[32,2,2,24,384]{4,3,2,1,0:T(8,128)(2,1)S(1)}, u32[]{:S(2)}, u32[]{:S(2)}) collective-permute-start(bf16[32,2,2,24,384]{4,3,2,1,0:T(8,128)(2,1)} %gather.3), channel_id=1, source_target_pairs={{0,32},{32,0},{1,33},{33,1},{2,34},{34,2},{3,35},{35,3},{4,36},{36... | collective-permute-start | bytes 7077896 | tf_op jit(solution)/shard_map/ppermute | solution.py:382

commit v3 on v0

v3 whole, which is shorter than its diff:
```python
import math

import jax
import jax.numpy as jnp
import numpy as np
from jax import lax
from jax.experimental import pallas as pl
from jax.experimental.pallas import tpu as pltpu
from jax.sharding import Mesh
from jax.sharding import PartitionSpec as P

COLUMN = ("x", "y", "zh", "zl")
ROWS = 384
SUBLANES = 8
GROUPS = 8


def make_tables(freqs, time):
    product = np.arange(1, freqs + 1)[:, None] * np.arange(time)[None, :] % time
    phase = product * (2.0 * math.pi / time)
    parts = np.stack([np.cos(phase), -np.sin(phase)], axis=1).reshape((2 * freqs, time))
    forward = (parts * math.sqrt(2.0 / time)).astype(np.float32)
    inverse = (parts / math.sqrt(freqs)).astype(np.float32)
    return (forward.astype(jnp.bfloat16), inverse.astype(jnp.bfloat16))


OWN_SLOT = 0
OTHER_SLOT = 2
OWN_MEMBER = 4
OTHER_MEMBER = 6
ENTRIES = 8


def deal(mirror_ref, table_ref):
    half = GROUPS // 2
    chip, core = lax.axis_index("zl"), lax.axis_index("core")
    mirror = [mirror_ref[g] for g in range(GROUPS)]
    zero, one = jnp.int32(0), jnp.int32(1)

    def flag(condition):
        return jnp.where(condition, one, zero)

    upper = [flag(m >= half) for m in mirror]
    within = [upper[g] if g >= half else 1 - upper[g] for g in range(GROUPS)]
    crossing = GROUPS - sum(within[1:], within[0])
    low = [jnp.minimum(m, g) for g, m in enumerate(mirror)]
    color, key = [], []
    for g in range(GROUPS):
        with_first = flag(mirror[g] - half * upper[g] == 0) if g % half else one
        color.append(
            jnp.where(
                crossing == GROUPS,
                flag(low[g] >= half // 2),
                jnp.where(crossing == half, 1 - within[g], 1 - with_first),
            )
        )
        key.append(jnp.where(within[g] == 1, g, low[g]))
    place = []
    for g in range(GROUPS):
        rank = zero
        for other in range(g // half * half, g // half * half + half):
            if other != g:
                rank = rank + flag(color[g] == color[other]) * flag(key[other] < key[g])
        place.append(2 * color[g] + rank)
    mine = [jnp.where(chip == 0, place[g], place[half + g]) for g in range(half)]
    for g in range(2):
        table_ref[OWN_SLOT + g] = jnp.where(core == 0, mine[g], mine[2 + g])
        table_ref[OTHER_SLOT + g] = jnp.where(core == 0, mine[2 + g], mine[g])
    mixed = jnp.where(chip == 0, flag(crossing == GROUPS), flag(crossing >= half))
    for j in range(2):
        table_ref[OWN_MEMBER + j] = jnp.where(mixed == 1, 2 * j + core, 2 * core + j)
        table_ref[OTHER_MEMBER + j] = jnp.where(mixed == 1, 2 * j + 1 - core, 2 * (1 - core) + j)


def params(limit):
    return pltpu.CompilerParams(vmem_limit_bytes=limit << 20)


SMEM = pl.BlockSpec(memory_space=pltpu.SMEM)
VMEM = pl.BlockSpec(memory_space=pltpu.VMEM)
ANY = pl.BlockSpec(memory_space=pl.ANY)
HBM = pl.BlockSpec(memory_space=pltpu.HBM)


def copy_all(pairs, sems):
    copies = [pltpu.make_async_copy(a, b, sems.at[i]) for i, (a, b) in enumerate(pairs)]
    for copy in copies:
        copy.start()
    for copy in copies:
        copy.wait()


def gather(table, whole, slots):
    blocks, _, parts, shots, width = whole.shape

    def body(table_ref, whole_ref, part_ref, sems):
        copy_all(
            [(whole_ref.at[:, table_ref[slots + j]], part_ref.at[:, j]) for j in range(2)], sems
        )

    return pl.pallas_call(
        body,
        in_specs=[SMEM, VMEM],
        out_specs=VMEM,
        out_shape=on_chip((blocks, 2, parts, shots, width)),
        scratch_shapes=[pltpu.SemaphoreType.DMA((2,))],
        compiler_params=params(8),
        name="gather",
    )(table, whole)


def scatter(table, part, whole, slots):
    def body(table_ref, part_ref, whole_ref, out_ref, sems):
        copy_all(
            [(part_ref.at[:, j], out_ref.at[:, table_ref[slots + j]]) for j in range(2)], sems
        )

    return pl.pallas_call(
        body,
        in_specs=[SMEM, VMEM, VMEM],
        out_specs=VMEM,
        out_shape=on_chip(whole.shape),
        scratch_shapes=[pltpu.SemaphoreType.DMA((2,))],
        input_output_aliases={2: 0},
        compiler_params=params(8),
        name="scatter",
    )(table, part, whole)


def on_chip(shape):
    return pltpu.VMEM(shape, jnp.bfloat16)


def two_shots(taps_ref):
    taps = taps_ref[...]
    blank = jnp.zeros_like(taps)
    return jnp.concatenate(
        [jnp.concatenate([taps, blank], axis=1), jnp.concatenate([blank, taps], axis=1)], axis=0
    )


def forward_transform(forward, records, mirror=None):
    groups, shots, recv, time = records.shape
    parts = forward.shape[0]
    width = recv // 2
    tiles = shots // SUBLANES
    count = groups if mirror is None else 2 * groups
    shape = (parts // 2, count, 2, shots, width)

    def body(forward_ref, records_ref, *refs):
        held, in_sems = refs[-2:]
        core = lax.axis_index("core")
        half = 1 - core if mirror is None else core
        start = pl.multiple_of(half * width, width)
        copies = []
        for i in range(groups * tiles):
            g, s = divmod(i, tiles)
            source = records_ref.at[g, pl.ds(s * SUBLANES, SUBLANES), pl.ds(start, width)]
            copies.append(pltpu.make_async_copy(source, held.at[i], in_sems.at[i]))
        for copy in copies:
            copy.start()
        two = two_shots(forward_ref)
        if mirror is None:
            (out_ref,) = refs[:-2]
            slots = range(groups)
        else:
            mirror_ref, out_ref, table_ref = refs[:-2]
            deal(mirror_ref, table_ref)
            slots = [table_ref[OWN_SLOT + g] for g in range(groups)]
        for i in range(groups * tiles):
            g, s = divmod(i, tiles)
            copies[i].wait()
            found = []
            for q in range(0, SUBLANES, 2):
                both = jnp.concatenate([held[i, q], held[i, q + 1]], axis=1)
                found.append(
                    lax.dot_general(
                        two, both, (((1,), (1,)), ((), ())), preferred_element_type=jnp.float32
                    )
                )
            found = jnp.concatenate(found, axis=0).reshape((SUBLANES, parts, width))
            found = jnp.transpose(found, (1, 0, 2)).reshape((parts // 2, 2, SUBLANES, width))
            window = slice(s * SUBLANES, (s + 1) * SUBLANES)
            out_ref[:, slots[g], :, window, :] = found.astype(jnp.bfloat16)

    scratch = [
        pltpu.VMEM((groups * tiles, SUBLANES, width, time), jnp.bfloat16),
        pltpu.SemaphoreType.DMA((groups * tiles,)),
    ]
    if mirror is None:
        return pl.pallas_call(
            body,
            in_specs=[VMEM, HBM],
            out_specs=VMEM,
            out_shape=on_chip(shape),
            scratch_shapes=scratch,
            compiler_params=params(16),
            name="forward",
        )(forward, records)
    return pl.pallas_call(
        body,
        in_specs=[VMEM, HBM, SMEM],
        out_specs=[VMEM, SMEM],
        out_shape=[on_chip(shape), jax.ShapeDtypeStruct((ENTRIES,), jnp.int32)],
        scratch_shapes=scratch,
        compiler_params=params(16),
        name="forward",
    )(forward, records, mirror)


def chain(table, surface, kept, got):
    blocks, _, parts, shots, width = kept.shape
    size = blocks * shots
    step = ROWS // shots

    def body(table_ref, scale_ref, kept_ref, got_ref, own_ref, other_ref, spectra_ref):
        core = lax.axis_index("core")
        slots = [table_ref[OWN_MEMBER + j] for j in range(2)]
        for value in range(2):

            @pl.when(core == value)
            def _():
                here = slice(value * width, (value + 1) * width)
                there = slice((1 - value) * width, (2 - value) * width)
                for j in range(2):
                    for c in range(2):
                        spectra_ref[j, c, :, here] = kept_ref[:, slots[j], c].reshape((size, width))
                        spectra_ref[j, c, :, there] = got_ref[:, j, c].reshape((size, width))

        scale = -scale_ref[...] / math.sqrt(2.0 * scale_ref.shape[-1])
        for j in range(2):
            both = spectra_ref[j, 0].astype(jnp.float32) + spectra_ref[j, 1].astype(jnp.float32)
            spectra_ref[j, 2] = both.astype(jnp.bfloat16)

        def dot(a, b):
            return jnp.dot(a, b, preferred_element_type=jnp.float32)

        def scaled(part):
            return (part * scale).astype(jnp.bfloat16)

        def times(left_re, left_im, mate):
            both = (left_re.astype(jnp.float32) + left_im.astype(jnp.float32)).astype(jnp.bfloat16)
            first = dot(left_re, spectra_ref[mate, 0])
            second = dot(left_im, spectra_ref[mate, 1])
            third = dot(both, spectra_ref[mate, 2])
            return first - second, third - first - second

        for j in range(2):
            for m in range(blocks // step):
                window = pl.ds(m * ROWS, ROWS)
                real_1, imag_1 = times(
                    scaled(spectra_ref[j, 0, window, :].astype(jnp.float32)),
                    scaled(spectra_ref[j, 1, window, :].astype(jnp.float32)),
                    1 - j,
                )
                real_2, imag_2 = times(scaled(real_1), scaled(imag_1), 1 - j)
                for c, total in enumerate((real_1 + real_2, imag_1 + imag_2)):
                    total = total.astype(jnp.bfloat16)
                    low = total[:, :width].reshape((step, shots, width))
                    high = total[:, width:].reshape((step, shots, width))

                    @pl.when(core == 0)
                    def _():
                        own_ref[pl.ds(m * step, step), slots[j], c] = low
                        other_ref[pl.ds(m * step, step), j, c] = high

                    @pl.when(core == 1)
                    def _():
                        own_ref[pl.ds(m * step, step), slots[j], c] = high
                        other_ref[pl.ds(m * step, step), j, c] = low

    return pl.pallas_call(
        body,
        in_specs=[SMEM, VMEM, VMEM, VMEM],
        out_specs=[VMEM, VMEM],
        out_shape=[on_chip(kept.shape), on_chip(got.shape)],
        scratch_shapes=[pltpu.VMEM((2, 3, size, 2 * width), jnp.bfloat16)],
        compiler_params=params(30),
        name="chain",
    )(table, surface, kept, got)


def inverse_transform(table, inverse, total, slots=None, whole=None):
    _, _, parts, shots, width = total.shape
    rows, time = inverse.shape
    tiles = shots // SUBLANES
    groups = 2

    def body(table_ref, inverse_ref, total_ref, *refs):
        out_ref, predicted, out_sems = refs[-3:]
        core = lax.axis_index("core")
        half = core if whole is None else 1 - core
        start = pl.multiple_of(half * width, width)
        two = two_shots(inverse_ref)
        copies = []
        for i in range(groups * tiles):
            g, s = divmod(i, tiles)
            slot = g if slots is None else table_ref[slots + g]
            block = total_ref[:, slot, :, s * SUBLANES : (s + 1) * SUBLANES, :]
            block = block.astype(jnp.float32).reshape((rows, SUBLANES, width))
            block = jnp.transpose(block, (1, 0, 2)).astype(jnp.bfloat16)
            for q in range(0, SUBLANES, 2):
                both = jnp.concatenate([block[q], block[q + 1]], axis=0)
                traces = lax.dot_general(
                    both, two, (((0,), (0,)), ((), ())), preferred_element_type=jnp.float32
                ).astype(jnp.bfloat16)
                predicted[i, q] = traces[:, :time]
                predicted[i, q + 1] = traces[:, time:]
            target = out_ref.at[g, pl.ds(s * SUBLANES, SUBLANES), pl.ds(start, width)]
            copies.append(pltpu.make_async_copy(predicted.at[i], target, out_sems.at[i]))
            copies[-1].start()
        for copy in copies:
            copy.wait()

    specs = [SMEM, VMEM, VMEM]
    operands = [table, inverse, total]
    aliases = {}
    if whole is not None:
        specs.append(ANY)
        operands.append(whole)
        aliases = {3: 0}
    return pl.pallas_call(
        body,
        in_specs=specs,
        out_specs=ANY,
        out_shape=jax.ShapeDtypeStruct((groups, shots, 2 * width, time), jnp.bfloat16),
        scratch_shapes=[
            pltpu.VMEM((groups * tiles, SUBLANES, width, time), jnp.bfloat16),
            pltpu.SemaphoreType.DMA((groups * tiles,)),
        ],
        input_output_aliases=aliases,
        compiler_params=params(16),
        name="inverse",
    )(*operands)


def stay(part):
    return pltpu.with_memory_space_constraint(part, pltpu.VMEM)


def other_core(part):
    return stay(lax.ppermute(part, "core", [(0, 1), (1, 0)]))


def exchange(chunks):
    blocks, count, parts, shots, width = chunks.shape
    chunks = chunks.reshape((2 * blocks, count // 2, parts, shots, width))
    chunks = lax.all_to_all(chunks, COLUMN, 0, 0, tiled=True)
    return stay(chunks.reshape((blocks, count, parts, shots, width)))


def local(records, surface, mirror):
    freqs = lax.axis_size("x") * lax.axis_size("y") * lax.axis_size("zh")
    forward, inverse = make_tables(freqs, records.shape[-1])

    sent = forward_transform(forward, records)
    chunks, table = forward_transform(forward, records, mirror)
    chunks = scatter(table, other_core(sent), chunks, OTHER_SLOT)
    chunks = exchange(chunks)
    got = other_core(gather(table, chunks, OTHER_MEMBER))
    own, other = chain(table, surface, chunks, got)
    chunks = scatter(table, other_core(other), own, OTHER_MEMBER)
    chunks = exchange(chunks)
    got = other_core(gather(table, chunks, OTHER_SLOT))
    predicted = inverse_transform(table, inverse, chunks, OWN_SLOT)
    return inverse_transform(table, inverse, got, None, predicted)


def solution(mesh):
    devices = mesh.devices.reshape((2, 2, 4, 4, 2))
    whole = Mesh(devices, ("zl", "core", "x", "y", "zh"))
    pair, shot = ("zl", "core"), ("x", "y", "zh")
    return jax.shard_map(
        local,
        mesh=whole,
        in_specs=(P(pair, shot, None, None), P(shot, None), P()),
        out_specs=P(pair, shot, None, None),
        check_vma=False,
    )
```

time: 427 us -> 182 us (0.43)
  waiting for transfers between devices: 163 us -> 9.41 us
  matrix products: 64.6 us -> 0 us
  local copies, waits for them, and re-layouts: 37.6 us -> 4.41 us
  Pallas kernels: 0 us -> 30.8 us
  between operations: 13.5 us -> 0.26 us
  other arithmetic: 13 us -> 0 us
  starting transfers between devices: 0.01 us -> 6.82 us
  blocking collectives: 135 us -> 130 us
    all_gather x1 -> x0, waiting for transfers between devices: 163 us -> none  [local(): piece = lax.all_gather(own_spec, 'pair', axis=0, tiled=True)]
    dot_general x11 -> x0, matrix products: 64.6 us -> none  [the longest x8 38.5 us: batch_dot(): jnp.einsum('kij,kjl->kil', left, right, preferred_element_type=jnp.float32)]
    pallas_call x0 -> x9, Pallas kernels: none -> 30.8 us  [the longest x1 14.2 us: chain(): pl.pallas_call(body, in_specs=[SMEM, VMEM, VMEM, VMEM], out_specs=[VMEM,...]
    unnamed x12 -> x10, local copies, waits for them, and re-layouts: 23.1 us -> 4.41 us
    convert_element_type x3 -> x0, other arithmetic: 12.9 us -> none  [the longest x1 5.38 us: chain_products(): left = (own_spec.astype(jnp.float32) * column_scale).astype(jnp.bfloat16)]
    convert_element_type x2 -> x0, local copies, waits for them, and re-layouts: 11.9 us -> none  [the longest x1 9.32 us: chain_products(): return total.astype(jnp.bfloat16)]
    ppermute x0 -> x4, waiting for transfers between devices: none -> 9.41 us  [other_core(): return stay(lax.ppermute(part, 'core', [(0, 1), (1, 0)]))]
    ppermute x0 -> x4, starting transfers between devices: none -> 6.82 us  [other_core(): return stay(lax.ppermute(part, 'core', [(0, 1), (1, 0)]))]
  transfers between devices with their start and end apart: 1 -> 4, of which waited for: 1 -> 4; matrix products, arithmetic and copies ran while one was open for 1% -> 0% of each run, Pallas kernels for 0% -> 4%
where the time goes in v3:
time: 182 us
  blocking collectives  130 us (71%)
  Pallas kernels  30.8 us (17%)
  waiting for transfers between devices  9.41 us (5%)
  starting transfers between devices  6.82 us (4%)
  local copies, waits for them, and re-layouts  4.41 us (2%)
    all_to_all x2, blocking collectives, exchange(): chunks = lax.all_to_all(chunks, COLUMN, 0, 0, tiled=True)  130 us
    pallas_call x1, Pallas kernels, chain(): pl.pallas_call(body, in_specs=[SMEM, VMEM, VMEM, VMEM], out_specs=[VMEM,...  14.2 us
    ppermute x4, waiting for transfers between devices, other_core(): return stay(lax.ppermute(part, 'core', [(0, 1), (1, 0)]))  9.41 us
    ppermute x4, starting transfers between devices, other_core(): return stay(lax.ppermute(part, 'core', [(0, 1), (1, 0)]))  6.82 us
    pallas_call x2, Pallas kernels, inverse_transform(): pl.pallas_call(body, in_specs=specs, out_specs=ANY, out_shape=jax.ShapeDt...  6.53 us
    unnamed x10, local copies, waits for them, and re-layouts  4.41 us
    pallas_call x1, Pallas kernels, forward_transform(): pl.pallas_call(body, in_specs=[VMEM, HBM, SMEM], out_specs=[VMEM, SMEM],...  3.93 us
  transfers between devices with their start and end apart: 4, of which 4 were waited for; matrix products, arithmetic and copies ran while one was open for 0% of the time, Pallas kernels for 4%

profile of v3, /device:TPU:1, one launch (start us, length us, event | category | flops | bytes accessed | tf_op | source)
XLA Modules:
  0.0 181.9 jit_solution(1783440001077016105)
XLA Ops:
  0.0 3.7 %copy-done = bf16[2,24,768,128]{3,2,1,0:T(8,128)(2,1)S(1)} copy-done((bf16[2,24,768,128]{3,2,1,0:T(8,128)(2,1)S(1)}, bf16[2,24,768,128]{3,2,1,0:T(8,128)(2,1)}, u32[]{:S(2)}) %copy-start) | copy-done | bytes 9437208
  3.7 0.7 copy-done.1
  4.4 3.1 %forward.3 = bf16[32,2,2,24,384]{4,3,2,1,0:T(8,128)(2,1)S(1)} custom-call(bf16[64,128]{1,0:T(8,128)(2,1)S(1)} %copy-done.1, bf16[2,24,768,128]{3,2,1,0:T(8,128)(2,1)S(1)} %copy-done), custom_call_target="tpu_custom_call" | custom-call | tf_op jit(solution)/shard_map/forward/pallas_call | solution.py:191
  7.5 1.5 collective-permute-start
  9.0 0.0 copy-done.4
  9.0 3.9 %forward.2 = (bf16[32,4,2,24,384]{4,3,2,1,0:T(8,128)(2,1)S(1)}, s32[8]{0:T(128)S(1)}) custom-call(bf16[64,128]{1,0:T(8,128)(2,1)S(1)} %copy-done.1, bf16[2,24,768,128]{3,2,1,0:T(8,128)(2,1)S(1)} %copy-done, s32[8]{0:T(128)S(1)} %copy-done.4), custom_call_target="tpu_custom_call" | custom-call | tf_op jit(solution)/shard_map/forward/pallas_call | solution.py:200
  13.0 0.2 collective-permute-done.part_ref
  13.2 0.8 scatter.2
  14.0 67.8 %all_to_all.10 = bf16[64,2,2,24,384]{4,3,2,1,0:T(8,128)(2,1)S(1)} all-to-all(bf16[64,2,2,24,384]{4,3,2,1,0:T(8,128)(2,1)S(1)} %bitcast.9), channel_id=1, replica_groups=mesh['zl'=2,'core'=2,'x'=4,'y'=4,'zh'=2] {'x','y','zh','zl'}, dimensions={0} | all-to-all | bytes 9437184 | tf_op jit(solution)/shard_map/all_to_all | solution.py:348
  81.8 0.7 gather.2
  82.5 2.3 %collective-permute-start.1 = (bf16[32,2,2,24,384]{4,3,2,1,0:T(8,128)(2,1)S(1)}, bf16[32,2,2,24,384]{4,3,2,1,0:T(8,128)(2,1)S(1)}, u32[]{:S(2)}, u32[]{:S(2)}) collective-permute-start(bf16[32,2,2,24,384]{4,3,2,1,0:T(8,128)(2,1)S(1)} %gather.2), channel_id=1, source_target_pairs={{0,32},{32,0},{1,33},{33,1},{2,34},{34,2},{3,35},{35,3},{4,36},{36... | collective-permute-start | bytes 7077896 | tf_op jit(solution)/shard_map/ppermute | solution.py:342
  84.9 4.2 %collective-permute-done.1.got_ref = bf16[32,2,2,24,384]{4,3,2,1,0:T(8,128)(2,1)S(1)} collective-permute-done((bf16[32,2,2,24,384]{4,3,2,1,0:T(8,128)(2,1)S(1)}, bf16[32,2,2,24,384]{4,3,2,1,0:T(8,128)(2,1)S(1)}, u32[]{:S(2)}, u32[]{:S(2)}) %collective-permute-start.1) | collective-permute-done | bytes 2359328 | tf_op jit(solution)/shard_map/ppermute | solution.py:342
  89.0 0.0 copy-done.3
  89.0 14.2 %chain.1 = (bf16[32,4,2,24,384]{4,3,2,1,0:T(8,128)(2,1)S(1)}, bf16[32,2,2,24,384]{4,3,2,1,0:T(8,128)(2,1)S(1)}) custom-call(s32[8]{0:T(128)S(1)} %get-tuple-element.9.table_ref, f32[1,768]{1,0:T(1,128)S(1)} %copy-done.3, bf16[32,4,2,24,384]{4,3,2,1,0:T(8,128)(2,1)S(1)} %bitcast.7, bf16[32,2,2,24,384]{4,3,2,1,0:T(8,128)(2,1)S(1)} %collective-permute-done.1.got_ref), custom_call_target="tpu_custom_call" | custom-call | tf_op jit(solution)/shard_map/chain/pallas_call | solution.py:272
  103.3 0.5 collective-permute-start.2
  103.7 4.2 %collective-permute-done.2.part_ref = bf16[32,2,2,24,384]{4,3,2,1,0:T(8,128)(2,1)S(1)} collective-permute-done((bf16[32,2,2,24,384]{4,3,2,1,0:T(8,128)(2,1)S(1)}, bf16[32,2,2,24,384]{4,3,2,1,0:T(8,128)(2,1)S(1)}, u32[]{:S(2)}, u32[]{:S(2)}) %collective-permute-start.2) | collective-permute-done | bytes 2359328 | tf_op jit(solution)/shard_map/ppermute | solution.py:342
  107.9 0.8 scatter.3
  108.7 62.3 %all_to_all.11 = bf16[64,2,2,24,384]{4,3,2,1,0:T(8,128)(2,1)S(1)} all-to-all(bf16[64,2,2,24,384]{4,3,2,1,0:T(8,128)(2,1)S(1)} %bitcast.8), channel_id=1, replica_groups=mesh['zl'=2,'core'=2,'x'=4,'y'=4,'zh'=2] {'x','y','zh','zl'}, dimensions={0} | all-to-all | bytes 9437184 | tf_op jit(solution)/shard_map/all_to_all | solution.py:348
  171.0 0.7 gather.3
  171.7 2.5 %collective-permute-start.3 = (bf16[32,2,2,24,384]{4,3,2,1,0:T(8,128)(2,1)S(1)}, bf16[32,2,2,24,384]{4,3,2,1,0:T(8,128)(2,1)S(1)}, u32[]{:S(2)}, u32[]{:S(2)}) collective-permute-start(bf16[32,2,2,24,384]{4,3,2,1,0:T(8,128)(2,1)S(1)} %gather.3), channel_id=1, source_target_pairs={{0,32},{32,0},{1,33},{33,1},{2,34},{34,2},{3,35},{35,3},{4,36},{36... | collective-permute-start | bytes 7077896 | tf_op jit(solution)/shard_map/ppermute | solution.py:342
  174.3 0.0 copy-done.2
  174.3 3.3 %inverse.2.refs_0_ = bf16[2,24,768,128]{3,2,1,0:T(8,128)(2,1)} custom-call(s32[8]{0:T(128)S(1)} %get-tuple-element.9.table_ref, bf16[64,128]{1,0:T(8,128)(2,1)S(1)} %copy-done.2, bf16[32,4,2,24,384]{4,3,2,1,0:T(8,128)(2,1)S(1)} %bitcast.5), custom_call_target="tpu_custom_call" | custom-call | tf_op jit(solution)/shard_map/inverse/pallas_call | solution.py:322
  177.5 0.9 collective-permute-done.3.total_ref
  178.4 3.3 %inverse.3 = bf16[2,24,768,128]{3,2,1,0:T(8,128)(2,1)} custom-call(s32[8]{0:T(128)S(1)} %get-tuple-element.9.table_ref, bf16[64,128]{1,0:T(8,128)(2,1)S(1)} %copy-done.2, bf16[32,2,2,24,384]{4,3,2,1,0:T(8,128)(2,1)S(1)} %collective-permute-done.3.total_ref, bf16[2,24,768,128]{3,2,1,0:T(8,128)(2,1)} %inverse.2.refs_0_), custom_call_target="tpu_custom_call", output_to_operand_aliasing={{}: (3, {})} | custom-call | tf_op jit(solution)/shard_map/inverse/pallas_call | solution.py:322
  (5 shorter events, 0.0 us)
Async XLA Ops:
  0.0 3.7 %copy-start = (bf16[2,24,768,128]{3,2,1,0:T(8,128)(2,1)S(1)}, bf16[2,24,768,128]{3,2,1,0:T(8,128)(2,1)}, u32[]{:S(2)}) copy-start(bf16[2,24,768,128]{3,2,1,0:T(8,128)(2,1)} %records_ref.3) | copy-start | bytes 28311556
  3.7 0.7 copy-start.1
  4.4 4.6 %copy-start.4 = (s32[8]{0:T(128)S(1)}, s32[8]{0:T(128)}, u32[]{:S(2)}) copy-start(s32[8]{0:T(128)} %refs_0_.1) | copy-start | bytes 100
  7.5 5.7 %collective-permute-start = (bf16[32,2,2,24,384]{4,3,2,1,0:T(8,128)(2,1)S(1)}, bf16[32,2,2,24,384]{4,3,2,1,0:T(8,128)(2,1)S(1)}, u32[]{:S(2)}, u32[]{:S(2)}) collective-permute-start(bf16[32,2,2,24,384]{4,3,2,1,0:T(8,128)(2,1)S(1)} %forward.3), channel_id=1, source_target_pairs={{0,32},{32,0},{1,33},{33,1},{2,34},{34,2},{3,35},{35,3},{4,36},{36... | collective-permute-start | bytes 7077896 | tf_op jit(solution)/shard_map/ppermute | solution.py:342
  81.8 7.2 %copy-start.3 = (f32[1,768]{1,0:T(1,128)S(1)}, f32[1,768]{1,0:T(1,128)}, u32[]{:S(2)}) copy-start(f32[1,768]{1,0:T(1,128)} %scale_ref.1) | copy-start | bytes 9220
  82.5 6.5 %collective-permute-start.1 = (bf16[32,2,2,24,384]{4,3,2,1,0:T(8,128)(2,1)S(1)}, bf16[32,2,2,24,384]{4,3,2,1,0:T(8,128)(2,1)S(1)}, u32[]{:S(2)}, u32[]{:S(2)}) collective-permute-start(bf16[32,2,2,24,384]{4,3,2,1,0:T(8,128)(2,1)S(1)} %gather.2), channel_id=1, source_target_pairs={{0,32},{32,0},{1,33},{33,1},{2,34},{34,2},{3,35},{35,3},{4,36},{36... | collective-permute-start | bytes 7077896 | tf_op jit(solution)/shard_map/ppermute | solution.py:342
  103.3 4.6 %collective-permute-start.2 = (bf16[32,2,2,24,384]{4,3,2,1,0:T(8,128)(2,1)S(1)}, bf16[32,2,2,24,384]{4,3,2,1,0:T(8,128)(2,1)S(1)}, u32[]{:S(2)}, u32[]{:S(2)}) collective-permute-start(bf16[32,2,2,24,384]{4,3,2,1,0:T(8,128)(2,1)S(1)} %get-tuple-element.11), channel_id=1, source_target_pairs={{0,32},{32,0},{1,33},{33,1},{2,34},{34,2},{3,35},{35,3},{4,36},{36... | collective-permute-start | bytes 7077896 | tf_op jit(solution)/shard_map/ppermute | solution.py:342
  171.0 3.3 %copy-start.2 = (bf16[64,128]{1,0:T(8,128)(2,1)S(1)}, bf16[64,128]{1,0:T(8,128)(2,1)}, u32[]{:S(2)}) copy-start(bf16[64,128]{1,0:T(8,128)(2,1)} %constant.5.clone.inverse_ref) | copy-start | bytes 49156
  171.7 6.7 %collective-permute-start.3 = (bf16[32,2,2,24,384]{4,3,2,1,0:T(8,128)(2,1)S(1)}, bf16[32,2,2,24,384]{4,3,2,1,0:T(8,128)(2,1)S(1)}, u32[]{:S(2)}, u32[]{:S(2)}) collective-permute-start(bf16[32,2,2,24,384]{4,3,2,1,0:T(8,128)(2,1)S(1)} %gather.3), channel_id=1, source_target_pairs={{0,32},{32,0},{1,33},{33,1},{2,34},{34,2},{3,35},{35,3},{4,36},{36... | collective-permute-start | bytes 7077896 | tf_op jit(solution)/shard_map/ppermute | solution.py:342

commit v4 on v3

--- a/solution.py
+++ b/solution.py
@@ -109,22 +109,29 @@
     )(table, whole)
 
 
-def scatter(table, part, whole, slots):
-    def body(table_ref, part_ref, whole_ref, out_ref, sems):
+def scatter(table, parts, whole, slots):
+    places = [(p, j) for p, part in enumerate(parts) for j in range(part.shape[1])]
+
+    def body(table_ref, *refs):
+        out_ref, sems = refs[-2:]
         copy_all(
-            [(part_ref.at[:, j], out_ref.at[:, table_ref[slots + j]]) for j in range(2)], sems
+            [
+                (refs[p].at[:, j], out_ref.at[:, table_ref[slots + i]])
+                for i, (p, j) in enumerate(places)
+            ],
+            sems,
         )
 
     return pl.pallas_call(
         body,
-        in_specs=[SMEM, VMEM, VMEM],
+        in_specs=[SMEM] + [VMEM] * (len(parts) + 1),
         out_specs=VMEM,
         out_shape=on_chip(whole.shape),
-        scratch_shapes=[pltpu.SemaphoreType.DMA((2,))],
-        input_output_aliases={2: 0},
+        scratch_shapes=[pltpu.SemaphoreType.DMA((len(places),))],
+        input_output_aliases={len(parts) + 1: 0},
         compiler_params=params(8),
         name="scatter",
-    )(table, part, whole)
+    )(table, *parts, whole)
 
 
 def on_chip(shape):
@@ -148,23 +155,26 @@
     shape = (parts // 2, count, 2, shots, width)
 
     def body(forward_ref, records_ref, *refs):
-        held, in_sems = refs[-2:]
+        held, taps, in_sems = refs[-3:]
         core = lax.axis_index("core")
         half = 1 - core if mirror is None else core
         start = pl.multiple_of(half * width, width)
         copies = []
+        table_copy = pltpu.make_async_copy(forward_ref, taps, in_sems.at[groups * tiles])
+        table_copy.start()
         for i in range(groups * tiles):
             g, s = divmod(i, tiles)
             source = records_ref.at[g, pl.ds(s * SUBLANES, SUBLANES), pl.ds(start, width)]
             copies.append(pltpu.make_async_copy(source, held.at[i], in_sems.at[i]))
         for copy in copies:
             copy.start()
-        two = two_shots(forward_ref)
+        table_copy.wait()
+        two = two_shots(taps)
         if mirror is None:
-            (out_ref,) = refs[:-2]
+            (out_ref,) = refs[:-3]
             slots = range(groups)
         else:
-            mirror_ref, out_ref, table_ref = refs[:-2]
+            mirror_ref, out_ref, table_ref = refs[:-3]
             deal(mirror_ref, table_ref)
             slots = [table_ref[OWN_SLOT + g] for g in range(groups)]
         for i in range(groups * tiles):
@@ -185,12 +195,13 @@
 
     scratch = [
         pltpu.VMEM((groups * tiles, SUBLANES, width, time), jnp.bfloat16),
-        pltpu.SemaphoreType.DMA((groups * tiles,)),
+        pltpu.VMEM((parts, time), jnp.bfloat16),
+        pltpu.SemaphoreType.DMA((groups * tiles + 1,)),
     ]
     if mirror is None:
         return pl.pallas_call(
             body,
-            in_specs=[VMEM, HBM],
+            in_specs=[HBM, HBM],
             out_specs=VMEM,
             out_shape=on_chip(shape),
             scratch_shapes=scratch,
@@ -199,7 +210,7 @@
         )(forward, records)
     return pl.pallas_call(
         body,
-        in_specs=[VMEM, HBM, SMEM],
+        in_specs=[HBM, HBM, SMEM],
         out_specs=[VMEM, SMEM],
         out_shape=[on_chip(shape), jax.ShapeDtypeStruct((ENTRIES,), jnp.int32)],
         scratch_shapes=scratch,
@@ -208,10 +219,44 @@
     )(forward, records, mirror)
 
 
-def chain(table, surface, kept, got):
+def multiply(j, slot, scale_ref, spectra_ref, own_ref, other_ref):
+    size, recv = spectra_ref.shape[-2:]
+    blocks, _, _, shots, width = other_ref.shape
+    step = ROWS // shots
+    core = lax.axis_index("core")
+    scale = -scale_ref[...] / math.sqrt(2.0 * recv)
+
+    def dot(a, b):
+        return jnp.dot(a, b, preferred_element_type=jnp.float32)
+
+    def scaled(part):
+        return (part * scale).astype(jnp.bfloat16)
+
+    def times(left_re, left_im):
+        both = (left_re.astype(jnp.float32) + left_im.astype(jnp.float32)).astype(jnp.bfloat16)
+        first = dot(left_re, spectra_ref[1 - j, 0])
+        second = dot(left_im, spectra_ref[1 - j, 1])
+        third = dot(both, spectra_ref[1 - j, 2])
+        return first - second, third - first - second
+
+    for m in range(blocks // step):
+        window = pl.ds(m * ROWS, ROWS)
+        real_1, imag_1 = times(
+            scaled(spectra_ref[j, 0, window, :].astype(jnp.float32)),
+            scaled(spectra_ref[j, 1, window, :].astype(jnp.float32)),
+        )
+        real_2, imag_2 = times(scaled(real_1), scaled(imag_1))
+        for c, total in enumerate((real_1 + real_2, imag_1 + imag_2)):
+            total = total.astype(jnp.bfloat16)
+            low = total[:, :width].reshape((step, shots, width))
+            high = total[:, width:].reshape((step, shots, width))
+            own_ref[pl.ds(m * step, step), slot, c] = jnp.where(core == 0, low, high)
+            other_ref[pl.ds(m * step, step), 0, c] = jnp.where(core == 0, high, low)
+
+
+def chain_first(table, surface, kept, got):
     blocks, _, parts, shots, width = kept.shape
     size = blocks * shots
-    step = ROWS // shots
 
     def body(table_ref, scale_ref, kept_ref, got_ref, own_ref, other_ref, spectra_ref):
         core = lax.axis_index("core")
@@ -227,57 +272,39 @@
                         spectra_ref[j, c, :, here] = kept_ref[:, slots[j], c].reshape((size, width))
                         spectra_ref[j, c, :, there] = got_ref[:, j, c].reshape((size, width))
 
-        scale = -scale_ref[...] / math.sqrt(2.0 * scale_ref.shape[-1])
         for j in range(2):
             both = spectra_ref[j, 0].astype(jnp.float32) + spectra_ref[j, 1].astype(jnp.float32)
             spectra_ref[j, 2] = both.astype(jnp.bfloat16)
-
-        def dot(a, b):
-            return jnp.dot(a, b, preferred_element_type=jnp.float32)
-
-        def scaled(part):
-            return (part * scale).astype(jnp.bfloat16)
-
-        def times(left_re, left_im, mate):
-            both = (left_re.astype(jnp.float32) + left_im.astype(jnp.float32)).astype(jnp.bfloat16)
-            first = dot(left_re, spectra_ref[mate, 0])
-            second = dot(left_im, spectra_ref[mate, 1])
-            third = dot(both, spectra_ref[mate, 2])
-            return first - second, third - first - second
-
-        for j in range(2):
-            for m in range(blocks // step):
-                window = pl.ds(m * ROWS, ROWS)
-                real_1, imag_1 = times(
-                    scaled(spectra_ref[j, 0, window, :].astype(jnp.float32)),
-                    scaled(spectra_ref[j, 1, window, :].astype(jnp.float32)),
-                    1 - j,
-                )
-                real_2, imag_2 = times(scaled(real_1), scaled(imag_1), 1 - j)
-                for c, total in enumerate((real_1 + real_2, imag_1 + imag_2)):
-                    total = total.astype(jnp.bfloat16)
-                    low = total[:, :width].reshape((step, shots, width))
-                    high = total[:, width:].reshape((step, shots, width))
-
-                    @pl.when(core == 0)
-                    def _():
-                        own_ref[pl.ds(m * step, step), slots[j], c] = low
-                        other_ref[pl.ds(m * step, step), j, c] = high
-
-                    @pl.when(core == 1)
-                    def _():
-                        own_ref[pl.ds(m * step, step), slots[j], c] = high
-                        other_ref[pl.ds(m * step, step), j, c] = low
+        multiply(0, slots[0], scale_ref, spectra_ref, own_ref, other_ref)
+
+    return pl.pallas_call(
+        body,
+        in_specs=[SMEM, VMEM, VMEM, VMEM],
+        out_specs=[VMEM, VMEM, VMEM],
+        out_shape=[
+            on_chip(kept.shape),
+            on_chip((blocks, 1, parts, shots, width)),
+            on_chip((2, 3, size, 2 * width)),
+        ],
+        compiler_params=params(20),
+        name="chain",
+    )(table, surface, kept, got)
+
+
+def chain_second(table, surface, spectra, own, other):
+    def body(table_ref, scale_ref, spectra_ref, first_ref, own_ref, other_ref):
+        slot = table_ref[OWN_MEMBER + 1]
+        multiply(1, slot, scale_ref, spectra_ref, own_ref, other_ref)
 
     return pl.pallas_call(
         body,
         in_specs=[SMEM, VMEM, VMEM, VMEM],
         out_specs=[VMEM, VMEM],
-        out_shape=[on_chip(kept.shape), on_chip(got.shape)],
-        scratch_shapes=[pltpu.VMEM((2, 3, size, 2 * width), jnp.bfloat16)],
-        compiler_params=params(30),
+        out_shape=[on_chip(own.shape), on_chip(other.shape)],
+        input_output_aliases={3: 0},
+        compiler_params=params(20),
         name="chain",
-    )(table, surface, kept, got)
+    )(table, surface, spectra, own)
 
 
 def inverse_transform(table, inverse, total, slots=None, whole=None):
@@ -352,14 +379,17 @@
 def local(records, surface, mirror):
     freqs = lax.axis_size("x") * lax.axis_size("y") * lax.axis_size("zh")
     forward, inverse = make_tables(freqs, records.shape[-1])
-
+    forward = pltpu.with_memory_space_constraint(forward, pltpu.HBM)
+    records = pltpu.with_memory_space_constraint(records, pltpu.HBM)
     sent = forward_transform(forward, records)
     chunks, table = forward_transform(forward, records, mirror)
-    chunks = scatter(table, other_core(sent), chunks, OTHER_SLOT)
+    chunks = scatter(table, [other_core(sent)], chunks, OTHER_SLOT)
     chunks = exchange(chunks)
     got = other_core(gather(table, chunks, OTHER_MEMBER))
-    own, other = chain(table, surface, chunks, got)
-    chunks = scatter(table, other_core(other), own, OTHER_MEMBER)
+    own, first, spectra = chain_first(table, surface, chunks, got)
+    first_got = other_core(first)
+    own, second = chain_second(table, surface, spectra, own, first)
+    chunks = scatter(table, [first_got, other_core(second)], own, OTHER_MEMBER)
     chunks = exchange(chunks)
     got = other_core(gather(table, chunks, OTHER_SLOT))
     predicted = inverse_transform(table, inverse, chunks, OWN_SLOT)

time: 182 us -> 179 us (0.984)
  local copies, waits for them, and re-layouts: 4.41 us -> 0.01 us
  Pallas kernels: 30.8 us -> 33.3 us
    unnamed x10 -> x6, local copies, waits for them, and re-layouts: 4.41 us -> 0.01 us
    pallas_call x5 -> x6, Pallas kernels: 22.8 us -> 25.3 us  [the longest x1 8.15 us: chain_first(): pl.pallas_call(body, in_specs=[SMEM, VMEM, VMEM, VMEM], out_specs=[VMEM,...]
    ppermute x4 -> x5, waiting for transfers between devices: 9.41 us -> 7.76 us  [other_core(): return stay(lax.ppermute(part, 'core', [(0, 1), (1, 0)]))]
    ppermute x4 -> x5, starting transfers between devices: 6.82 us -> 5.92 us  [other_core(): return stay(lax.ppermute(part, 'core', [(0, 1), (1, 0)]))]
  transfers between devices with their start and end apart: 4 -> 5, of which waited for: 4 -> 3; matrix products, arithmetic and copies ran while one was open for 0% -> 0% of each run, Pallas kernels for 4% -> 8%
where the time goes in v4:
time: 179 us; the launch traced here: 178 us
  blocking collectives  131 us (73%)
  Pallas kernels  33.3 us (19%)
  waiting for transfers between devices  7.76 us (4%)
  starting transfers between devices  5.92 us (3%)
    all_to_all x2, blocking collectives, exchange(): chunks = lax.all_to_all(chunks, COLUMN, 0, 0, tiled=True)  131 us
    pallas_call x1, Pallas kernels, chain_first(): pl.pallas_call(body, in_specs=[SMEM, VMEM, VMEM, VMEM], out_specs=[VMEM,...  8.15 us
    ppermute x5, waiting for transfers between devices, other_core(): return stay(lax.ppermute(part, 'core', [(0, 1), (1, 0)]))  7.76 us
    pallas_call x1, Pallas kernels, chain_second(): pl.pallas_call(body, in_specs=[SMEM, VMEM, VMEM, VMEM], out_specs=[VMEM,...  6.96 us
    pallas_call x2, Pallas kernels, inverse_transform(): pl.pallas_call(body, in_specs=specs, out_specs=ANY, out_shape=jax.ShapeDt...  6.53 us
    ppermute x5, starting transfers between devices, other_core(): return stay(lax.ppermute(part, 'core', [(0, 1), (1, 0)]))  5.92 us
    pallas_call x1, Pallas kernels, forward_transform(): pl.pallas_call(body, in_specs=[HBM, HBM, SMEM], out_specs=[VMEM, SMEM], o...  4.65 us
    pallas_call x1, Pallas kernels, forward_transform(): pl.pallas_call(body, in_specs=[HBM, HBM], out_specs=VMEM, out_shape=on_ch...  3.98 us
  transfers between devices with their start and end apart: 5, of which 3 were waited for; matrix products, arithmetic and copies ran while one was open for 0% of the time, Pallas kernels for 8%

profile of v4, /device:TPU:1, one launch (start us, length us, event | category | flops | bytes accessed | tf_op | source)
XLA Modules:
  0.0 178.3 jit_solution(18193011283182905052)
XLA Ops:
  0.0 4.0 %forward.3 = bf16[32,2,2,24,384]{4,3,2,1,0:T(8,128)(2,1)S(1)} custom-call(bf16[64,128]{1,0:T(8,128)(2,1)} %constant.4.clone.forward_ref, bf16[2,24,768,128]{3,2,1,0:T(8,128)(2,1)} %records_ref.3), custom_call_target="tpu_custom_call" | custom-call | tf_op jit(solution)/shard_map/forward/pallas_call | solution.py:202
  4.0 1.5 collective-permute-start
  5.5 0.0 copy-done.2
  5.5 4.7 %forward.2 = (bf16[32,4,2,24,384]{4,3,2,1,0:T(8,128)(2,1)S(1)}, s32[8]{0:T(128)S(1)}) custom-call(bf16[64,128]{1,0:T(8,128)(2,1)} %constant.4.clone.forward_ref, bf16[2,24,768,128]{3,2,1,0:T(8,128)(2,1)} %records_ref.3, s32[8]{0:T(128)S(1)} %copy-done.2), custom_call_target="tpu_custom_call" | custom-call | tf_op jit(solution)/shard_map/forward/pallas_call | solution.py:211
  10.2 0.0 collective-permute-done.refs_0_
  10.2 0.8 scatter.2
  10.9 68.3 %all_to_all.10 = bf16[64,2,2,24,384]{4,3,2,1,0:T(8,128)(2,1)S(1)} all-to-all(bf16[64,2,2,24,384]{4,3,2,1,0:T(8,128)(2,1)S(1)} %bitcast.9), channel_id=1, replica_groups=mesh['zl'=2,'core'=2,'x'=4,'y'=4,'zh'=2] {'x','y','zh','zl'}, dimensions={0} | all-to-all | bytes 9437184 | tf_op jit(solution)/shard_map/all_to_all | solution.py:375
  79.2 0.7 gather.2
  80.0 1.8 %collective-permute-start.1 = (bf16[32,2,2,24,384]{4,3,2,1,0:T(8,128)(2,1)S(1)}, bf16[32,2,2,24,384]{4,3,2,1,0:T(8,128)(2,1)S(1)}, u32[]{:S(2)}, u32[]{:S(2)}) collective-permute-start(bf16[32,2,2,24,384]{4,3,2,1,0:T(8,128)(2,1)S(1)} %gather.2), channel_id=1, source_target_pairs={{0,32},{32,0},{1,33},{33,1},{2,34},{34,2},{3,35},{35,3},{4,36},{36... | collective-permute-start | bytes 7077896 | tf_op jit(solution)/shard_map/ppermute | solution.py:369
  81.7 4.2 %collective-permute-done.1.got_ref = bf16[32,2,2,24,384]{4,3,2,1,0:T(8,128)(2,1)S(1)} collective-permute-done((bf16[32,2,2,24,384]{4,3,2,1,0:T(8,128)(2,1)S(1)}, bf16[32,2,2,24,384]{4,3,2,1,0:T(8,128)(2,1)S(1)}, u32[]{:S(2)}, u32[]{:S(2)}) %collective-permute-start.1) | collective-permute-done | bytes 2359328 | tf_op jit(solution)/shard_map/ppermute | solution.py:369
  85.9 8.1 %chain.2 = (bf16[32,4,2,24,384]{4,3,2,1,0:T(8,128)(2,1)S(1)}, bf16[32,1,2,24,384]{4,3,2,1,0:T(8,128)(2,1)S(1)}, bf16[2,3,768,768]{3,2,1,0:T(8,128)(2,1)S(1)}) custom-call(s32[8]{0:T(128)S(1)} %get-tuple-element.12.table_ref, f32[1,768]{1,0:T(1,128)S(1)} %copy-done.1, bf16[32,4,2,24,384]{4,3,2,1,0:T(8,128)(2,1)S(1)} %bitcast.7, ...), custom_call_target="tpu_custom_call" | custom-call | tf_op jit(solution)/shard_map/chain/pallas_call | solution.py:280
  94.1 0.5 collective-permute-start.2
  94.5 7.0 %chain.3 = (bf16[32,4,2,24,384]{4,3,2,1,0:T(8,128)(2,1)S(1)}, bf16[32,1,2,24,384]{4,3,2,1,0:T(8,128)(2,1)S(1)}) custom-call(s32[8]{0:T(128)S(1)} %get-tuple-element.12.table_ref, f32[1,768]{1,0:T(1,128)S(1)} %copy-done.1, bf16[2,3,768,768]{3,2,1,0:T(8,128)(2,1)S(1)} %get-tuple-element.15.spectra_ref, ...), custom_call_target="tpu_custom_call", output_to_operand_aliasing={{0}: (3, {})} | custom-call | tf_op jit(solution)/shard_map/chain/pallas_call | solution.py:299
  101.5 0.2 collective-permute-start.3
  101.7 0.0 collective-permute-done.2.refs_0_
  101.7 2.7 %collective-permute-done.3.refs_1_ = bf16[32,1,2,24,384]{4,3,2,1,0:T(8,128)(2,1)S(1)} collective-permute-done((bf16[32,1,2,24,384]{4,3,2,1,0:T(8,128)(2,1)S(1)}, bf16[32,1,2,24,384]{4,3,2,1,0:T(8,128)(2,1)S(1)}, u32[]{:S(2)}, u32[]{:S(2)}) %collective-permute-start.3) | collective-permute-done | bytes 1179680 | tf_op jit(solution)/shard_map/ppermute | solution.py:369
  104.4 0.8 scatter.3
  105.2 62.8 %all_to_all.11 = bf16[64,2,2,24,384]{4,3,2,1,0:T(8,128)(2,1)S(1)} all-to-all(bf16[64,2,2,24,384]{4,3,2,1,0:T(8,128)(2,1)S(1)} %bitcast.8), channel_id=1, replica_groups=mesh['zl'=2,'core'=2,'x'=4,'y'=4,'zh'=2] {'x','y','zh','zl'}, dimensions={0} | all-to-all | bytes 9437184 | tf_op jit(solution)/shard_map/all_to_all | solution.py:375
  168.0 0.7 gather.3
  168.7 2.0 %collective-permute-start.4 = (bf16[32,2,2,24,384]{4,3,2,1,0:T(8,128)(2,1)S(1)}, bf16[32,2,2,24,384]{4,3,2,1,0:T(8,128)(2,1)S(1)}, u32[]{:S(2)}, u32[]{:S(2)}) collective-permute-start(bf16[32,2,2,24,384]{4,3,2,1,0:T(8,128)(2,1)S(1)} %gather.3), channel_id=1, source_target_pairs={{0,32},{32,0},{1,33},{33,1},{2,34},{34,2},{3,35},{35,3},{4,36},{36... | collective-permute-start | bytes 7077896 | tf_op jit(solution)/shard_map/ppermute | solution.py:369
  170.7 0.0 copy-done
  170.7 3.3 %inverse.2.refs_0_ = bf16[2,24,768,128]{3,2,1,0:T(8,128)(2,1)} custom-call(s32[8]{0:T(128)S(1)} %get-tuple-element.12.table_ref, bf16[64,128]{1,0:T(8,128)(2,1)S(1)} %copy-done, bf16[32,4,2,24,384]{4,3,2,1,0:T(8,128)(2,1)S(1)} %bitcast.5), custom_call_target="tpu_custom_call" | custom-call | tf_op jit(solution)/shard_map/inverse/pallas_call | solution.py:349
  173.9 0.9 collective-permute-done.4.total_ref
  174.8 3.3 %inverse.3 = bf16[2,24,768,128]{3,2,1,0:T(8,128)(2,1)} custom-call(s32[8]{0:T(128)S(1)} %get-tuple-element.12.table_ref, bf16[64,128]{1,0:T(8,128)(2,1)S(1)} %copy-done, bf16[32,2,2,24,384]{4,3,2,1,0:T(8,128)(2,1)S(1)} %collective-permute-done.4.total_ref, bf16[2,24,768,128]{3,2,1,0:T(8,128)(2,1)} %inverse.2.refs_0_), custom_call_target="tpu_custom_call", output_to_operand_aliasing={{}: (3, {})} | custom-call | tf_op jit(solution)/shard_map/inverse/pallas_call | solution.py:349
  (4 shorter events, 0.0 us)
Async XLA Ops:
  0.0 5.5 %copy-start.2 = (s32[8]{0:T(128)S(1)}, s32[8]{0:T(128)}, u32[]{:S(2)}) copy-start(s32[8]{0:T(128)} %refs_0_.1) | copy-start | bytes 100
  4.0 6.2 %collective-permute-start = (bf16[32,2,2,24,384]{4,3,2,1,0:T(8,128)(2,1)S(1)}, bf16[32,2,2,24,384]{4,3,2,1,0:T(8,128)(2,1)S(1)}, u32[]{:S(2)}, u32[]{:S(2)}) collective-permute-start(bf16[32,2,2,24,384]{4,3,2,1,0:T(8,128)(2,1)S(1)} %forward.3), channel_id=1, source_target_pairs={{0,32},{32,0},{1,33},{33,1},{2,34},{34,2},{3,35},{35,3},{4,36},{36... | collective-permute-start | bytes 7077896 | tf_op jit(solution)/shard_map/ppermute | solution.py:369
  79.2 6.7 %copy-start.1 = (f32[1,768]{1,0:T(1,128)S(1)}, f32[1,768]{1,0:T(1,128)}, u32[]{:S(2)}) copy-start(f32[1,768]{1,0:T(1,128)} %scale_ref.3) | copy-start | bytes 9220
  80.0 6.0 %collective-permute-start.1 = (bf16[32,2,2,24,384]{4,3,2,1,0:T(8,128)(2,1)S(1)}, bf16[32,2,2,24,384]{4,3,2,1,0:T(8,128)(2,1)S(1)}, u32[]{:S(2)}, u32[]{:S(2)}) collective-permute-start(bf16[32,2,2,24,384]{4,3,2,1,0:T(8,128)(2,1)S(1)} %gather.2), channel_id=1, source_target_pairs={{0,32},{32,0},{1,33},{33,1},{2,34},{34,2},{3,35},{35,3},{4,36},{36... | collective-permute-start | bytes 7077896 | tf_op jit(solution)/shard_map/ppermute | solution.py:369
  94.1 7.6 %collective-permute-start.2 = (bf16[32,1,2,24,384]{4,3,2,1,0:T(8,128)(2,1)S(1)}, bf16[32,1,2,24,384]{4,3,2,1,0:T(8,128)(2,1)S(1)}, u32[]{:S(2)}, u32[]{:S(2)}) collective-permute-start(bf16[32,1,2,24,384]{4,3,2,1,0:T(8,128)(2,1)S(1)} %get-tuple-element.14), channel_id=1, source_target_pairs={{0,32},{32,0},{1,33},{33,1},{2,34},{34,2},{3,35},{35,3},{4,36},{36... | collective-permute-start | bytes 3538952 | tf_op jit(solution)/shard_map/ppermute | solution.py:369
  101.5 2.9 %collective-permute-start.3 = (bf16[32,1,2,24,384]{4,3,2,1,0:T(8,128)(2,1)S(1)}, bf16[32,1,2,24,384]{4,3,2,1,0:T(8,128)(2,1)S(1)}, u32[]{:S(2)}, u32[]{:S(2)}) collective-permute-start(bf16[32,1,2,24,384]{4,3,2,1,0:T(8,128)(2,1)S(1)} %get-tuple-element.17), channel_id=1, source_target_pairs={{0,32},{32,0},{1,33},{33,1},{2,34},{34,2},{3,35},{35,3},{4,36},{36... | collective-permute-start | bytes 3538952 | tf_op jit(solution)/shard_map/ppermute | solution.py:369
  168.0 2.7 %copy-start = (bf16[64,128]{1,0:T(8,128)(2,1)S(1)}, bf16[64,128]{1,0:T(8,128)(2,1)}, u32[]{:S(2)}) copy-start(bf16[64,128]{1,0:T(8,128)(2,1)} %constant.5.clone.inverse_ref) | copy-start | bytes 49156
  168.7 6.1 %collective-permute-start.4 = (bf16[32,2,2,24,384]{4,3,2,1,0:T(8,128)(2,1)S(1)}, bf16[32,2,2,24,384]{4,3,2,1,0:T(8,128)(2,1)S(1)}, u32[]{:S(2)}, u32[]{:S(2)}) collective-permute-start(bf16[32,2,2,24,384]{4,3,2,1,0:T(8,128)(2,1)S(1)} %gather.3), channel_id=1, source_target_pairs={{0,32},{32,0},{1,33},{33,1},{2,34},{34,2},{3,35},{35,3},{4,36},{36... | collective-permute-start | bytes 7077896 | tf_op jit(solution)/shard_map/ppermute | solution.py:369

commit v5 on v4

--- a/solution.py
+++ b/solution.py
@@ -12,6 +12,7 @@
 COLUMN = ("x", "y", "zh", "zl")
 ROWS = 384
 SUBLANES = 8
+AHEAD = 2
 GROUPS = 8
 
 
@@ -90,20 +91,22 @@
         copy.wait()
 
 
-def gather(table, whole, slots):
+def gather(table, whole, entries):
     blocks, _, parts, shots, width = whole.shape
+    count = len(entries)
 
     def body(table_ref, whole_ref, part_ref, sems):
         copy_all(
-            [(whole_ref.at[:, table_ref[slots + j]], part_ref.at[:, j]) for j in range(2)], sems
+            [(whole_ref.at[:, table_ref[e]], part_ref.at[:, j]) for j, e in enumerate(entries)],
+            sems,
         )
 
     return pl.pallas_call(
         body,
         in_specs=[SMEM, VMEM],
         out_specs=VMEM,
-        out_shape=on_chip((blocks, 2, parts, shots, width)),
-        scratch_shapes=[pltpu.SemaphoreType.DMA((2,))],
+        out_shape=on_chip((blocks, count, parts, shots, width)),
+        scratch_shapes=[pltpu.SemaphoreType.DMA((count,))],
         compiler_params=params(8),
         name="gather",
     )(table, whole)
@@ -146,43 +149,55 @@
     )
 
 
-def forward_transform(forward, records, mirror=None):
+def forward_transform(forward, records, mirror=None, ahead=None):
     groups, shots, recv, time = records.shape
     parts = forward.shape[0]
     width = recv // 2
     tiles = shots // SUBLANES
     count = groups if mirror is None else 2 * groups
     shape = (parts // 2, count, 2, shots, width)
+    early = (AHEAD, SUBLANES, width, time)
 
     def body(forward_ref, records_ref, *refs):
         held, taps, in_sems = refs[-3:]
         core = lax.axis_index("core")
-        half = 1 - core if mirror is None else core
-        start = pl.multiple_of(half * width, width)
-        copies = []
+
+        def fetch(i, half, target, sem):
+            g, s = divmod(i, tiles)
+            start = pl.multiple_of(half * width, width)
+            source = records_ref.at[g, pl.ds(s * SUBLANES, SUBLANES), pl.ds(start, width)]
+            copy = pltpu.make_async_copy(source, target, in_sems.at[sem])
+            copy.start()
+            return copy
+
         table_copy = pltpu.make_async_copy(forward_ref, taps, in_sems.at[groups * tiles])
         table_copy.start()
+        waiting = {}
+        if mirror is None:
+            out_ref, ahead_ref = refs[:-3]
+            for i in range(groups * tiles):
+                waiting[i] = fetch(i, 1 - core, held.at[i], i)
+            late = [
+                fetch(i, core, ahead_ref.at[i], groups * tiles + 1 + i) for i in range(AHEAD)
+            ]
+            slots = range(groups)
+        else:
+            mirror_ref, ahead_ref, out_ref, table_ref = refs[:-3]
+            for i in range(AHEAD, groups * tiles):
+                waiting[i] = fetch(i, core, held.at[i], i)
+            late = []
+            deal(mirror_ref, table_ref)
+            slots = [table_ref[OWN_SLOT + g] for g in range(groups)]
+        table_copy.wait()
+        two = two_shots(taps)
         for i in range(groups * tiles):
             g, s = divmod(i, tiles)
-            source = records_ref.at[g, pl.ds(s * SUBLANES, SUBLANES), pl.ds(start, width)]
-            copies.append(pltpu.make_async_copy(source, held.at[i], in_sems.at[i]))
-        for copy in copies:
-            copy.start()
-        table_copy.wait()
-        two = two_shots(taps)
-        if mirror is None:
-            (out_ref,) = refs[:-3]
-            slots = range(groups)
-        else:
-            mirror_ref, out_ref, table_ref = refs[:-3]
-            deal(mirror_ref, table_ref)
-            slots = [table_ref[OWN_SLOT + g] for g in range(groups)]
-        for i in range(groups * tiles):
-            g, s = divmod(i, tiles)
-            copies[i].wait()
+            if i in waiting:
+                waiting[i].wait()
+            block_ref = held if i in waiting else ahead_ref
             found = []
             for q in range(0, SUBLANES, 2):
-                both = jnp.concatenate([held[i, q], held[i, q + 1]], axis=1)
+                both = jnp.concatenate([block_ref[i, q], block_ref[i, q + 1]], axis=1)
                 found.append(
                     lax.dot_general(
                         two, both, (((1,), (1,)), ((), ())), preferred_element_type=jnp.float32
@@ -192,31 +207,33 @@
             found = jnp.transpose(found, (1, 0, 2)).reshape((parts // 2, 2, SUBLANES, width))
             window = slice(s * SUBLANES, (s + 1) * SUBLANES)
             out_ref[:, slots[g], :, window, :] = found.astype(jnp.bfloat16)
+        for copy in late:
+            copy.wait()
 
     scratch = [
         pltpu.VMEM((groups * tiles, SUBLANES, width, time), jnp.bfloat16),
         pltpu.VMEM((parts, time), jnp.bfloat16),
-        pltpu.SemaphoreType.DMA((groups * tiles + 1,)),
+        pltpu.SemaphoreType.DMA((groups * tiles + 1 + AHEAD,)),
     ]
     if mirror is None:
         return pl.pallas_call(
             body,
             in_specs=[HBM, HBM],
-            out_specs=VMEM,
-            out_shape=on_chip(shape),
+            out_specs=[VMEM, VMEM],
+            out_shape=[on_chip(shape), on_chip(early)],
             scratch_shapes=scratch,
             compiler_params=params(16),
             name="forward",
         )(forward, records)
     return pl.pallas_call(
         body,
-        in_specs=[HBM, HBM, SMEM],
+        in_specs=[HBM, HBM, SMEM, VMEM],
         out_specs=[VMEM, SMEM],
         out_shape=[on_chip(shape), jax.ShapeDtypeStruct((ENTRIES,), jnp.int32)],
         scratch_shapes=scratch,
         compiler_params=params(16),
         name="forward",
-    )(forward, records, mirror)
+    )(forward, records, mirror, ahead)
 
 
 def multiply(j, slot, scale_ref, spectra_ref, own_ref, other_ref):
@@ -233,7 +250,7 @@
         return (part * scale).astype(jnp.bfloat16)
 
     def times(left_re, left_im):
-        both = (left_re.astype(jnp.float32) + left_im.astype(jnp.float32)).astype(jnp.bfloat16)
+        both = left_re + left_im
         first = dot(left_re, spectra_ref[1 - j, 0])
         second = dot(left_im, spectra_ref[1 - j, 1])
         third = dot(both, spectra_ref[1 - j, 2])
@@ -251,10 +268,10 @@
             low = total[:, :width].reshape((step, shots, width))
             high = total[:, width:].reshape((step, shots, width))
             own_ref[pl.ds(m * step, step), slot, c] = jnp.where(core == 0, low, high)
-            other_ref[pl.ds(m * step, step), 0, c] = jnp.where(core == 0, high, low)
-
-
-def chain_first(table, surface, kept, got):
+            other_ref[pl.ds(m * step, step), j, c] = jnp.where(core == 0, high, low)
+
+
+def chain(table, surface, kept, got):
     blocks, _, parts, shots, width = kept.shape
     size = blocks * shots
 
@@ -273,45 +290,26 @@
                         spectra_ref[j, c, :, there] = got_ref[:, j, c].reshape((size, width))
 
         for j in range(2):
-            both = spectra_ref[j, 0].astype(jnp.float32) + spectra_ref[j, 1].astype(jnp.float32)
-            spectra_ref[j, 2] = both.astype(jnp.bfloat16)
-        multiply(0, slots[0], scale_ref, spectra_ref, own_ref, other_ref)
-
-    return pl.pallas_call(
-        body,
-        in_specs=[SMEM, VMEM, VMEM, VMEM],
-        out_specs=[VMEM, VMEM, VMEM],
-        out_shape=[
-            on_chip(kept.shape),
-            on_chip((blocks, 1, parts, shots, width)),
-            on_chip((2, 3, size, 2 * width)),
-        ],
-        compiler_params=params(20),
-        name="chain",
-    )(table, surface, kept, got)
-
-
-def chain_second(table, surface, spectra, own, other):
-    def body(table_ref, scale_ref, spectra_ref, first_ref, own_ref, other_ref):
-        slot = table_ref[OWN_MEMBER + 1]
-        multiply(1, slot, scale_ref, spectra_ref, own_ref, other_ref)
+            spectra_ref[j, 2] = spectra_ref[j, 0] + spectra_ref[j, 1]
+        for j in range(2):
+            multiply(j, slots[j], scale_ref, spectra_ref, own_ref, other_ref)
 
     return pl.pallas_call(
         body,
         in_specs=[SMEM, VMEM, VMEM, VMEM],
         out_specs=[VMEM, VMEM],
-        out_shape=[on_chip(own.shape), on_chip(other.shape)],
-        input_output_aliases={3: 0},
-        compiler_params=params(20),
+        out_shape=[on_chip(kept.shape), on_chip(got.shape)],
+        scratch_shapes=[pltpu.VMEM((2, 3, size, 2 * width), jnp.bfloat16)],
+        compiler_params=params(30),
         name="chain",
-    )(table, surface, spectra, own)
-
-
-def inverse_transform(table, inverse, total, slots=None, whole=None):
+    )(table, surface, kept, got)
+
+
+def inverse_transform(table, inverse, total, groups, whole=None):
     _, _, parts, shots, width = total.shape
     rows, time = inverse.shape
     tiles = shots // SUBLANES
-    groups = 2
+    count = len(groups)
 
     def body(table_ref, inverse_ref, total_ref, *refs):
         out_ref, predicted, out_sems = refs[-3:]
@@ -320,9 +318,10 @@
         start = pl.multiple_of(half * width, width)
         two = two_shots(inverse_ref)
         copies = []
-        for i in range(groups * tiles):
-            g, s = divmod(i, tiles)
-            slot = g if slots is None else table_ref[slots + g]
+        for i in range(count * tiles):
+            n, s = divmod(i, tiles)
+            g = groups[n]
+            slot = table_ref[OWN_SLOT + g] if whole is None else n
             block = total_ref[:, slot, :, s * SUBLANES : (s + 1) * SUBLANES, :]
             block = block.astype(jnp.float32).reshape((rows, SUBLANES, width))
             block = jnp.transpose(block, (1, 0, 2)).astype(jnp.bfloat16)
@@ -350,10 +349,10 @@
         body,
         in_specs=specs,
         out_specs=ANY,
-        out_shape=jax.ShapeDtypeStruct((groups, shots, 2 * width, time), jnp.bfloat16),
+        out_shape=jax.ShapeDtypeStruct((2, shots, 2 * width, time), jnp.bfloat16),
         scratch_shapes=[
-            pltpu.VMEM((groups * tiles, SUBLANES, width, time), jnp.bfloat16),
-            pltpu.SemaphoreType.DMA((groups * tiles,)),
+            pltpu.VMEM((count * tiles, SUBLANES, width, time), jnp.bfloat16),
+            pltpu.SemaphoreType.DMA((count * tiles,)),
         ],
         input_output_aliases=aliases,
         compiler_params=params(16),
@@ -381,19 +380,19 @@
     forward, inverse = make_tables(freqs, records.shape[-1])
     forward = pltpu.with_memory_space_constraint(forward, pltpu.HBM)
     records = pltpu.with_memory_space_constraint(records, pltpu.HBM)
-    sent = forward_transform(forward, records)
-    chunks, table = forward_transform(forward, records, mirror)
+    sent, ahead = forward_transform(forward, records)
+    chunks, table = forward_transform(forward, records, mirror, ahead)
     chunks = scatter(table, [other_core(sent)], chunks, OTHER_SLOT)
     chunks = exchange(chunks)
-    got = other_core(gather(table, chunks, OTHER_MEMBER))
-    own, first, spectra = chain_first(table, surface, chunks, got)
-    first_got = other_core(first)
-    own, second = chain_second(table, surface, spectra, own, first)
-    chunks = scatter(table, [first_got, other_core(second)], own, OTHER_MEMBER)
+    got = other_core(gather(table, chunks, [OTHER_MEMBER, OTHER_MEMBER + 1]))
+    own, other = chain(table, surface, chunks, got)
+    chunks = scatter(table, [other_core(other)], own, OTHER_MEMBER)
     chunks = exchange(chunks)
-    got = other_core(gather(table, chunks, OTHER_SLOT))
-    predicted = inverse_transform(table, inverse, chunks, OWN_SLOT)
-    return inverse_transform(table, inverse, got, None, predicted)
+    got = [other_core(gather(table, chunks, [OTHER_SLOT + g])) for g in range(2)]
+    predicted = inverse_transform(table, inverse, chunks, [0, 1])
+    for g in range(2):
+        predicted = inverse_transform(table, inverse, got[g], [g], predicted)
+    return predicted
 
 
 def solution(mesh):

time: 179 us -> 179 us (level)
    pallas_call x4 -> x3, Pallas kernels: 23.7 us -> 21.1 us  [the longest x1 13.1 us: chain(): pl.pallas_call(body, in_specs=[SMEM, VMEM, VMEM, VMEM], out_specs=[VMEM,...]
    pallas_call x2 -> x3, Pallas kernels: 6.53 us -> 8.19 us  [inverse_transform(): pl.pallas_call(body, in_specs=specs, out_specs=ANY, out_shape=jax.ShapeDt...]
  transfers between devices with their start and end apart: 5 -> 5, of which waited for: 3 -> 3; matrix products, arithmetic and copies ran while one was open for 0% -> 0% of each run, Pallas kernels for 8% -> 6%
where the time goes in v5:
time: 179 us
  blocking collectives  130 us (73%)
  Pallas kernels  32.9 us (18%)
  waiting for transfers between devices  8.44 us (5%)
  starting transfers between devices  6.91 us (4%)
    all_to_all x2, blocking collectives, exchange(): chunks = lax.all_to_all(chunks, COLUMN, 0, 0, tiled=True)  130 us
    pallas_call x1, Pallas kernels, chain(): pl.pallas_call(body, in_specs=[SMEM, VMEM, VMEM, VMEM], out_specs=[VMEM,...  13.1 us
    ppermute x5, waiting for transfers between devices, other_core(): return stay(lax.ppermute(part, 'core', [(0, 1), (1, 0)]))  8.44 us
    pallas_call x3, Pallas kernels, inverse_transform(): pl.pallas_call(body, in_specs=specs, out_specs=ANY, out_shape=jax.ShapeDt...  8.19 us
    ppermute x5, starting transfers between devices, other_core(): return stay(lax.ppermute(part, 'core', [(0, 1), (1, 0)]))  6.91 us
    pallas_call x1, Pallas kernels, forward_transform(): pl.pallas_call(body, in_specs=[HBM, HBM, SMEM, VMEM], out_specs=[VMEM, SM...  4.03 us
    pallas_call x1, Pallas kernels, forward_transform(): pl.pallas_call(body, in_specs=[HBM, HBM], out_specs=[VMEM, VMEM], out_sha...  4.01 us
  transfers between devices with their start and end apart: 5, of which 3 were waited for; matrix products, arithmetic and copies ran while one was open for 0% of the time, Pallas kernels for 6%

profile of v5, /device:TPU:1, one launch (start us, length us, event | category | flops | bytes accessed | tf_op | source)
XLA Modules:
  0.0 178.7 jit_solution(11840857821452541635)
XLA Ops:
  0.0 4.0 %forward.2 = (bf16[32,2,2,24,384]{4,3,2,1,0:T(8,128)(2,1)S(1)}, bf16[2,8,384,128]{3,2,1,0:T(8,128)(2,1)S(1)}) custom-call(bf16[64,128]{1,0:T(8,128)(2,1)} %constant.4.clone.forward_ref, bf16[2,24,768,128]{3,2,1,0:T(8,128)(2,1)} %records_ref.3), custom_call_target="tpu_custom_call" | custom-call | tf_op jit(solution)/shard_map/forward/pallas_call | solution.py:219
  4.0 1.5 collective-permute-start
  5.5 4.0 %forward.3 = (bf16[32,4,2,24,384]{4,3,2,1,0:T(8,128)(2,1)S(1)}, s32[8]{0:T(128)S(1)}) custom-call(bf16[64,128]{1,0:T(8,128)(2,1)} %constant.4.clone.forward_ref, bf16[2,24,768,128]{3,2,1,0:T(8,128)(2,1)} %records_ref.3, s32[8]{0:T(128)S(1)} %copy-done.2, bf16[2,8,384,128]{3,2,1,0:T(8,128)(2,1)S(1)} %get-tuple-element.11.refs_1_), custom_call_target="tpu_custom_call" | custom-call | tf_op jit(solution)/shard_map/forward/pallas_call | solution.py:228
  9.6 0.1 collective-permute-done.refs_0_
  9.7 0.8 scatter.2
  10.4 67.8 %all_to_all.10 = bf16[64,2,2,24,384]{4,3,2,1,0:T(8,128)(2,1)S(1)} all-to-all(bf16[64,2,2,24,384]{4,3,2,1,0:T(8,128)(2,1)S(1)} %bitcast.10), channel_id=1, replica_groups=mesh['zl'=2,'core'=2,'x'=4,'y'=4,'zh'=2] {'x','y','zh','zl'}, dimensions={0} | all-to-all | bytes 9437184 | tf_op jit(solution)/shard_map/all_to_all | solution.py:374
  78.3 0.7 gather.3
  79.0 2.3 %collective-permute-start.1 = (bf16[32,2,2,24,384]{4,3,2,1,0:T(8,128)(2,1)S(1)}, bf16[32,2,2,24,384]{4,3,2,1,0:T(8,128)(2,1)S(1)}, u32[]{:S(2)}, u32[]{:S(2)}) collective-permute-start(bf16[32,2,2,24,384]{4,3,2,1,0:T(8,128)(2,1)S(1)} %gather.3), channel_id=1, source_target_pairs={{0,32},{32,0},{1,33},{33,1},{2,34},{34,2},{3,35},{35,3},{4,36},{36... | collective-permute-start | bytes 7077896 | tf_op jit(solution)/shard_map/ppermute | solution.py:368
  81.3 4.2 %collective-permute-done.1.got_ref = bf16[32,2,2,24,384]{4,3,2,1,0:T(8,128)(2,1)S(1)} collective-permute-done((bf16[32,2,2,24,384]{4,3,2,1,0:T(8,128)(2,1)S(1)}, bf16[32,2,2,24,384]{4,3,2,1,0:T(8,128)(2,1)S(1)}, u32[]{:S(2)}, u32[]{:S(2)}) %collective-permute-start.1) | collective-permute-done | bytes 2359328 | tf_op jit(solution)/shard_map/ppermute | solution.py:368
  85.5 13.1 %chain.1 = (bf16[32,4,2,24,384]{4,3,2,1,0:T(8,128)(2,1)S(1)}, bf16[32,2,2,24,384]{4,3,2,1,0:T(8,128)(2,1)S(1)}) custom-call(s32[8]{0:T(128)S(1)} %get-tuple-element.12.table_ref, f32[1,768]{1,0:T(1,128)S(1)} %copy-done.1, bf16[32,4,2,24,384]{4,3,2,1,0:T(8,128)(2,1)S(1)} %bitcast.8, bf16[32,2,2,24,384]{4,3,2,1,0:T(8,128)(2,1)S(1)} %collective-permute-done.1.got_ref), custom_call_target="tpu_custom_call" | custom-call | tf_op jit(solution)/shard_map/chain/pallas_call | solution.py:297
  98.6 0.5 collective-permute-start.2
  99.1 4.2 %collective-permute-done.2.refs_0_ = bf16[32,2,2,24,384]{4,3,2,1,0:T(8,128)(2,1)S(1)} collective-permute-done((bf16[32,2,2,24,384]{4,3,2,1,0:T(8,128)(2,1)S(1)}, bf16[32,2,2,24,384]{4,3,2,1,0:T(8,128)(2,1)S(1)}, u32[]{:S(2)}, u32[]{:S(2)}) %collective-permute-start.2) | collective-permute-done | bytes 2359328 | tf_op jit(solution)/shard_map/ppermute | solution.py:368
  103.2 0.8 scatter.3
  104.0 62.3 %all_to_all.11 = bf16[64,2,2,24,384]{4,3,2,1,0:T(8,128)(2,1)S(1)} all-to-all(bf16[64,2,2,24,384]{4,3,2,1,0:T(8,128)(2,1)S(1)} %bitcast.9), channel_id=1, replica_groups=mesh['zl'=2,'core'=2,'x'=4,'y'=4,'zh'=2] {'x','y','zh','zl'}, dimensions={0} | all-to-all | bytes 9437184 | tf_op jit(solution)/shard_map/all_to_all | solution.py:374
  166.3 0.6 gather.5
  166.9 0.0 copy-start
  166.9 2.5 %collective-permute-start.4 = (bf16[32,1,2,24,384]{4,3,2,1,0:T(8,128)(2,1)S(1)}, bf16[32,1,2,24,384]{4,3,2,1,0:T(8,128)(2,1)S(1)}, u32[]{:S(2)}, u32[]{:S(2)}) collective-permute-start(bf16[32,1,2,24,384]{4,3,2,1,0:T(8,128)(2,1)S(1)} %gather.5), channel_id=1, source_target_pairs={{0,32},{32,0},{1,33},{33,1},{2,34},{34,2},{3,35},{35,3},{4,36},{36... | collective-permute-start | bytes 3538952 | tf_op jit(solution)/shard_map/ppermute | solution.py:368
  169.5 0.6 gather.4
  170.1 0.1 collective-permute-start.3
  170.2 3.3 %inverse.3.refs_0_ = bf16[2,24,768,128]{3,2,1,0:T(8,128)(2,1)} custom-call(s32[8]{0:T(128)S(1)} %get-tuple-element.12.table_ref, bf16[64,128]{1,0:T(8,128)(2,1)S(1)} %copy-done, bf16[32,4,2,24,384]{4,3,2,1,0:T(8,128)(2,1)S(1)} %bitcast.6), custom_call_target="tpu_custom_call" | custom-call | tf_op jit(solution)/shard_map/inverse/pallas_call | solution.py:348
  173.5 0.0 collective-permute-done.4.total_ref
  173.5 2.5 %inverse.4.refs_0_ = bf16[2,24,768,128]{3,2,1,0:T(8,128)(2,1)} custom-call(s32[8]{0:T(128)S(1)} %get-tuple-element.12.table_ref, bf16[64,128]{1,0:T(8,128)(2,1)S(1)} %copy-done, bf16[32,1,2,24,384]{4,3,2,1,0:T(8,128)(2,1)S(1)} %collective-permute-done.4.total_ref, bf16[2,24,768,128]{3,2,1,0:T(8,128)(2,1)} %inverse.3.refs_0_), custom_call_target="tpu_custom_call", output_to_operand_aliasing={{}: (3, {})} | custom-call | tf_op jit(solution)/shard_map/inverse/pallas_call | solution.py:348
  176.0 0.0 collective-permute-done.3.total_ref
  176.0 2.5 %inverse.5 = bf16[2,24,768,128]{3,2,1,0:T(8,128)(2,1)} custom-call(s32[8]{0:T(128)S(1)} %get-tuple-element.12.table_ref, bf16[64,128]{1,0:T(8,128)(2,1)S(1)} %copy-done, bf16[32,1,2,24,384]{4,3,2,1,0:T(8,128)(2,1)S(1)} %collective-permute-done.3.total_ref, bf16[2,24,768,128]{3,2,1,0:T(8,128)(2,1)} %inverse.4.refs_0_), custom_call_target="tpu_custom_call", output_to_operand_aliasing={{}: (3, {})} | custom-call | tf_op jit(solution)/shard_map/inverse/pallas_call | solution.py:348
  (5 shorter events, 0.0 us)
Async XLA Ops:
  0.0 5.5 %copy-start.2 = (s32[8]{0:T(128)S(1)}, s32[8]{0:T(128)}, u32[]{:S(2)}) copy-start(s32[8]{0:T(128)} %refs_0_.1) | copy-start | bytes 100
  4.0 5.7 %collective-permute-start = (bf16[32,2,2,24,384]{4,3,2,1,0:T(8,128)(2,1)S(1)}, bf16[32,2,2,24,384]{4,3,2,1,0:T(8,128)(2,1)S(1)}, u32[]{:S(2)}, u32[]{:S(2)}) collective-permute-start(bf16[32,2,2,24,384]{4,3,2,1,0:T(8,128)(2,1)S(1)} %get-tuple-element.13), channel_id=1, source_target_pairs={{0,32},{32,0},{1,33},{33,1},{2,34},{34,2},{3,35},{35,3},{4,36},{36... | collective-permute-start | bytes 7077896 | tf_op jit(solution)/shard_map/ppermute | solution.py:368
  78.3 7.2 %copy-start.1 = (f32[1,768]{1,0:T(1,128)S(1)}, f32[1,768]{1,0:T(1,128)}, u32[]{:S(2)}) copy-start(f32[1,768]{1,0:T(1,128)} %scale_ref.1) | copy-start | bytes 9220
  79.0 6.5 %collective-permute-start.1 = (bf16[32,2,2,24,384]{4,3,2,1,0:T(8,128)(2,1)S(1)}, bf16[32,2,2,24,384]{4,3,2,1,0:T(8,128)(2,1)S(1)}, u32[]{:S(2)}, u32[]{:S(2)}) collective-permute-start(bf16[32,2,2,24,384]{4,3,2,1,0:T(8,128)(2,1)S(1)} %gather.3), channel_id=1, source_target_pairs={{0,32},{32,0},{1,33},{33,1},{2,34},{34,2},{3,35},{35,3},{4,36},{36... | collective-permute-start | bytes 7077896 | tf_op jit(solution)/shard_map/ppermute | solution.py:368
  98.6 4.6 %collective-permute-start.2 = (bf16[32,2,2,24,384]{4,3,2,1,0:T(8,128)(2,1)S(1)}, bf16[32,2,2,24,384]{4,3,2,1,0:T(8,128)(2,1)S(1)}, u32[]{:S(2)}, u32[]{:S(2)}) collective-permute-start(bf16[32,2,2,24,384]{4,3,2,1,0:T(8,128)(2,1)S(1)} %get-tuple-element.15), channel_id=1, source_target_pairs={{0,32},{32,0},{1,33},{33,1},{2,34},{34,2},{3,35},{35,3},{4,36},{36... | collective-permute-start | bytes 7077896 | tf_op jit(solution)/shard_map/ppermute | solution.py:368
  166.9 3.3 %copy-start = (bf16[64,128]{1,0:T(8,128)(2,1)S(1)}, bf16[64,128]{1,0:T(8,128)(2,1)}, u32[]{:S(2)}) copy-start(bf16[64,128]{1,0:T(8,128)(2,1)} %constant.5.clone.inverse_ref) | copy-start | bytes 49156
  166.9 6.6 %collective-permute-start.4 = (bf16[32,1,2,24,384]{4,3,2,1,0:T(8,128)(2,1)S(1)}, bf16[32,1,2,24,384]{4,3,2,1,0:T(8,128)(2,1)S(1)}, u32[]{:S(2)}, u32[]{:S(2)}) collective-permute-start(bf16[32,1,2,24,384]{4,3,2,1,0:T(8,128)(2,1)S(1)} %gather.5), channel_id=1, source_target_pairs={{0,32},{32,0},{1,33},{33,1},{2,34},{34,2},{3,35},{35,3},{4,36},{36... | collective-permute-start | bytes 3538952 | tf_op jit(solution)/shard_map/ppermute | solution.py:368
  170.1 5.9 %collective-permute-start.3 = (bf16[32,1,2,24,384]{4,3,2,1,0:T(8,128)(2,1)S(1)}, bf16[32,1,2,24,384]{4,3,2,1,0:T(8,128)(2,1)S(1)}, u32[]{:S(2)}, u32[]{:S(2)}) collective-permute-start(bf16[32,1,2,24,384]{4,3,2,1,0:T(8,128)(2,1)S(1)} %gather.4), channel_id=1, source_target_pairs={{0,32},{32,0},{1,33},{33,1},{2,34},{34,2},{3,35},{35,3},{4,36},{36... | collective-permute-start | bytes 3538952 | tf_op jit(solution)/shard_map/ppermute | solution.py:368

commit v6 on v5

--- a/solution.py
+++ b/solution.py
@@ -388,11 +388,9 @@
     own, other = chain(table, surface, chunks, got)
     chunks = scatter(table, [other_core(other)], own, OTHER_MEMBER)
     chunks = exchange(chunks)
-    got = [other_core(gather(table, chunks, [OTHER_SLOT + g])) for g in range(2)]
+    got = other_core(gather(table, chunks, [OTHER_SLOT, OTHER_SLOT + 1]))
     predicted = inverse_transform(table, inverse, chunks, [0, 1])
-    for g in range(2):
-        predicted = inverse_transform(table, inverse, got[g], [g], predicted)
-    return predicted
+    return inverse_transform(table, inverse, got, [0, 1], predicted)
 
 
 def solution(mesh):

time: 179 us -> 177 us (0.989)
  Pallas kernels: 32.9 us -> 30.7 us
    pallas_call x3 -> x2, Pallas kernels: 8.19 us -> 6.53 us  [inverse_transform(): pl.pallas_call(body, in_specs=specs, out_specs=ANY, out_shape=jax.ShapeDt...]
    ppermute x5 -> x4, waiting for transfers between devices: 8.44 us -> 9.32 us  [other_core(): return stay(lax.ppermute(part, 'core', [(0, 1), (1, 0)]))]
    ppermute x5 -> x4, starting transfers between devices: 6.91 us -> 6.82 us  [other_core(): return stay(lax.ppermute(part, 'core', [(0, 1), (1, 0)]))]
  transfers between devices with their start and end apart: 5 -> 4, of which waited for: 3 -> 4; matrix products, arithmetic and copies ran while one was open for 0% -> 0% of each run, Pallas kernels for 6% -> 4%
where the time goes in v6:
time: 177 us
  blocking collectives  130 us (73%)
  Pallas kernels  30.7 us (17%)
  waiting for transfers between devices  9.32 us (5%)
  starting transfers between devices  6.82 us (4%)
    all_to_all x2, blocking collectives, exchange(): chunks = lax.all_to_all(chunks, COLUMN, 0, 0, tiled=True)  130 us
    pallas_call x1, Pallas kernels, chain(): pl.pallas_call(body, in_specs=[SMEM, VMEM, VMEM, VMEM], out_specs=[VMEM,...  13.1 us
    ppermute x4, waiting for transfers between devices, other_core(): return stay(lax.ppermute(part, 'core', [(0, 1), (1, 0)]))  9.32 us
    ppermute x4, starting transfers between devices, other_core(): return stay(lax.ppermute(part, 'core', [(0, 1), (1, 0)]))  6.82 us
    pallas_call x2, Pallas kernels, inverse_transform(): pl.pallas_call(body, in_specs=specs, out_specs=ANY, out_shape=jax.ShapeDt...  6.53 us
    pallas_call x1, Pallas kernels, forward_transform(): pl.pallas_call(body, in_specs=[HBM, HBM, SMEM, VMEM], out_specs=[VMEM, SM...  4.04 us
    pallas_call x1, Pallas kernels, forward_transform(): pl.pallas_call(body, in_specs=[HBM, HBM], out_specs=[VMEM, VMEM], out_sha...  4.01 us
  transfers between devices with their start and end apart: 4, of which 4 were waited for; matrix products, arithmetic and copies ran while one was open for 0% of the time, Pallas kernels for 4%

profile of v6, /device:TPU:1, one launch (start us, length us, event | category | flops | bytes accessed | tf_op | source)
XLA Modules:
  0.0 177.1 jit_solution(11795235027121816842)
XLA Ops:
  0.0 0.0 copy-start.2
  0.0 4.0 %forward.2 = (bf16[32,2,2,24,384]{4,3,2,1,0:T(8,128)(2,1)S(1)}, bf16[2,8,384,128]{3,2,1,0:T(8,128)(2,1)S(1)}) custom-call(bf16[64,128]{1,0:T(8,128)(2,1)} %constant.4.clone.forward_ref, bf16[2,24,768,128]{3,2,1,0:T(8,128)(2,1)} %records_ref.3), custom_call_target="tpu_custom_call" | custom-call | tf_op jit(solution)/shard_map/forward/pallas_call | solution.py:219
  4.0 1.5 collective-permute-start
  5.5 0.0 copy-done.2
  5.5 4.0 %forward.3 = (bf16[32,4,2,24,384]{4,3,2,1,0:T(8,128)(2,1)S(1)}, s32[8]{0:T(128)S(1)}) custom-call(bf16[64,128]{1,0:T(8,128)(2,1)} %constant.4.clone.forward_ref, bf16[2,24,768,128]{3,2,1,0:T(8,128)(2,1)} %records_ref.3, s32[8]{0:T(128)S(1)} %copy-done.2, bf16[2,8,384,128]{3,2,1,0:T(8,128)(2,1)S(1)} %get-tuple-element.11.refs_1_), custom_call_target="tpu_custom_call" | custom-call | tf_op jit(solution)/shard_map/forward/pallas_call | solution.py:228
  9.6 0.1 collective-permute-done.refs_0_
  9.7 0.8 scatter.2
  10.4 67.8 %all_to_all.10 = bf16[64,2,2,24,384]{4,3,2,1,0:T(8,128)(2,1)S(1)} all-to-all(bf16[64,2,2,24,384]{4,3,2,1,0:T(8,128)(2,1)S(1)} %bitcast.9), channel_id=1, replica_groups=mesh['zl'=2,'core'=2,'x'=4,'y'=4,'zh'=2] {'x','y','zh','zl'}, dimensions={0} | all-to-all | bytes 9437184 | tf_op jit(solution)/shard_map/all_to_all | solution.py:374
  78.2 0.0 copy-start.1
  78.2 0.7 gather.2
  79.0 2.3 %collective-permute-start.1 = (bf16[32,2,2,24,384]{4,3,2,1,0:T(8,128)(2,1)S(1)}, bf16[32,2,2,24,384]{4,3,2,1,0:T(8,128)(2,1)S(1)}, u32[]{:S(2)}, u32[]{:S(2)}) collective-permute-start(bf16[32,2,2,24,384]{4,3,2,1,0:T(8,128)(2,1)S(1)} %gather.2), channel_id=1, source_target_pairs={{0,32},{32,0},{1,33},{33,1},{2,34},{34,2},{3,35},{35,3},{4,36},{36... | collective-permute-start | bytes 7077896 | tf_op jit(solution)/shard_map/ppermute | solution.py:368
  81.3 4.2 %collective-permute-done.1.got_ref = bf16[32,2,2,24,384]{4,3,2,1,0:T(8,128)(2,1)S(1)} collective-permute-done((bf16[32,2,2,24,384]{4,3,2,1,0:T(8,128)(2,1)S(1)}, bf16[32,2,2,24,384]{4,3,2,1,0:T(8,128)(2,1)S(1)}, u32[]{:S(2)}, u32[]{:S(2)}) %collective-permute-start.1) | collective-permute-done | bytes 2359328 | tf_op jit(solution)/shard_map/ppermute | solution.py:368
  85.5 0.0 copy-done.1
  85.5 13.1 %chain.1 = (bf16[32,4,2,24,384]{4,3,2,1,0:T(8,128)(2,1)S(1)}, bf16[32,2,2,24,384]{4,3,2,1,0:T(8,128)(2,1)S(1)}) custom-call(s32[8]{0:T(128)S(1)} %get-tuple-element.12.table_ref, f32[1,768]{1,0:T(1,128)S(1)} %copy-done.1, bf16[32,4,2,24,384]{4,3,2,1,0:T(8,128)(2,1)S(1)} %bitcast.7, bf16[32,2,2,24,384]{4,3,2,1,0:T(8,128)(2,1)S(1)} %collective-permute-done.1.got_ref), custom_call_target="tpu_custom_call" | custom-call | tf_op jit(solution)/shard_map/chain/pallas_call | solution.py:297
  98.6 0.5 collective-permute-start.2
  99.0 4.2 %collective-permute-done.2.refs_0_ = bf16[32,2,2,24,384]{4,3,2,1,0:T(8,128)(2,1)S(1)} collective-permute-done((bf16[32,2,2,24,384]{4,3,2,1,0:T(8,128)(2,1)S(1)}, bf16[32,2,2,24,384]{4,3,2,1,0:T(8,128)(2,1)S(1)}, u32[]{:S(2)}, u32[]{:S(2)}) %collective-permute-start.2) | collective-permute-done | bytes 2359328 | tf_op jit(solution)/shard_map/ppermute | solution.py:368
  103.2 0.8 scatter.3
  104.0 62.2 %all_to_all.11 = bf16[64,2,2,24,384]{4,3,2,1,0:T(8,128)(2,1)S(1)} all-to-all(bf16[64,2,2,24,384]{4,3,2,1,0:T(8,128)(2,1)S(1)} %bitcast.8), channel_id=1, replica_groups=mesh['zl'=2,'core'=2,'x'=4,'y'=4,'zh'=2] {'x','y','zh','zl'}, dimensions={0} | all-to-all | bytes 9437184 | tf_op jit(solution)/shard_map/all_to_all | solution.py:374
  166.2 0.7 gather.3
  167.0 2.5 %collective-permute-start.3 = (bf16[32,2,2,24,384]{4,3,2,1,0:T(8,128)(2,1)S(1)}, bf16[32,2,2,24,384]{4,3,2,1,0:T(8,128)(2,1)S(1)}, u32[]{:S(2)}, u32[]{:S(2)}) collective-permute-start(bf16[32,2,2,24,384]{4,3,2,1,0:T(8,128)(2,1)S(1)} %gather.3), channel_id=1, source_target_pairs={{0,32},{32,0},{1,33},{33,1},{2,34},{34,2},{3,35},{35,3},{4,36},{36... | collective-permute-start | bytes 7077896 | tf_op jit(solution)/shard_map/ppermute | solution.py:368
  169.5 0.0 copy-done
  169.5 3.3 %inverse.2.refs_0_ = bf16[2,24,768,128]{3,2,1,0:T(8,128)(2,1)} custom-call(s32[8]{0:T(128)S(1)} %get-tuple-element.12.table_ref, bf16[64,128]{1,0:T(8,128)(2,1)S(1)} %copy-done, bf16[32,4,2,24,384]{4,3,2,1,0:T(8,128)(2,1)S(1)} %bitcast.5), custom_call_target="tpu_custom_call" | custom-call | tf_op jit(solution)/shard_map/inverse/pallas_call | solution.py:348
  172.8 0.9 collective-permute-done.3.total_ref
  173.7 3.3 %inverse.3 = bf16[2,24,768,128]{3,2,1,0:T(8,128)(2,1)} custom-call(s32[8]{0:T(128)S(1)} %get-tuple-element.12.table_ref, bf16[64,128]{1,0:T(8,128)(2,1)S(1)} %copy-done, bf16[32,2,2,24,384]{4,3,2,1,0:T(8,128)(2,1)S(1)} %collective-permute-done.3.total_ref, bf16[2,24,768,128]{3,2,1,0:T(8,128)(2,1)} %inverse.2.refs_0_), custom_call_target="tpu_custom_call", output_to_operand_aliasing={{}: (3, {})} | custom-call | tf_op jit(solution)/shard_map/inverse/pallas_call | solution.py:348
  (1 shorter events, 0.0 us)
Async XLA Ops:
  0.0 5.5 %copy-start.2 = (s32[8]{0:T(128)S(1)}, s32[8]{0:T(128)}, u32[]{:S(2)}) copy-start(s32[8]{0:T(128)} %refs_0_.1) | copy-start | bytes 100
  4.0 5.7 %collective-permute-start = (bf16[32,2,2,24,384]{4,3,2,1,0:T(8,128)(2,1)S(1)}, bf16[32,2,2,24,384]{4,3,2,1,0:T(8,128)(2,1)S(1)}, u32[]{:S(2)}, u32[]{:S(2)}) collective-permute-start(bf16[32,2,2,24,384]{4,3,2,1,0:T(8,128)(2,1)S(1)} %get-tuple-element.13), channel_id=1, source_target_pairs={{0,32},{32,0},{1,33},{33,1},{2,34},{34,2},{3,35},{35,3},{4,36},{36... | collective-permute-start | bytes 7077896 | tf_op jit(solution)/shard_map/ppermute | solution.py:368
  78.2 7.2 %copy-start.1 = (f32[1,768]{1,0:T(1,128)S(1)}, f32[1,768]{1,0:T(1,128)}, u32[]{:S(2)}) copy-start(f32[1,768]{1,0:T(1,128)} %scale_ref.1) | copy-start | bytes 9220
  79.0 6.5 %collective-permute-start.1 = (bf16[32,2,2,24,384]{4,3,2,1,0:T(8,128)(2,1)S(1)}, bf16[32,2,2,24,384]{4,3,2,1,0:T(8,128)(2,1)S(1)}, u32[]{:S(2)}, u32[]{:S(2)}) collective-permute-start(bf16[32,2,2,24,384]{4,3,2,1,0:T(8,128)(2,1)S(1)} %gather.2), channel_id=1, source_target_pairs={{0,32},{32,0},{1,33},{33,1},{2,34},{34,2},{3,35},{35,3},{4,36},{36... | collective-permute-start | bytes 7077896 | tf_op jit(solution)/shard_map/ppermute | solution.py:368
  98.6 4.6 %collective-permute-start.2 = (bf16[32,2,2,24,384]{4,3,2,1,0:T(8,128)(2,1)S(1)}, bf16[32,2,2,24,384]{4,3,2,1,0:T(8,128)(2,1)S(1)}, u32[]{:S(2)}, u32[]{:S(2)}) collective-permute-start(bf16[32,2,2,24,384]{4,3,2,1,0:T(8,128)(2,1)S(1)} %get-tuple-element.15), channel_id=1, source_target_pairs={{0,32},{32,0},{1,33},{33,1},{2,34},{34,2},{3,35},{35,3},{4,36},{36... | collective-permute-start | bytes 7077896 | tf_op jit(solution)/shard_map/ppermute | solution.py:368
  166.2 3.3 %copy-start = (bf16[64,128]{1,0:T(8,128)(2,1)S(1)}, bf16[64,128]{1,0:T(8,128)(2,1)}, u32[]{:S(2)}) copy-start(bf16[64,128]{1,0:T(8,128)(2,1)} %constant.5.clone.inverse_ref) | copy-start | bytes 49156
  167.0 6.7 %collective-permute-start.3 = (bf16[32,2,2,24,384]{4,3,2,1,0:T(8,128)(2,1)S(1)}, bf16[32,2,2,24,384]{4,3,2,1,0:T(8,128)(2,1)S(1)}, u32[]{:S(2)}, u32[]{:S(2)}) collective-permute-start(bf16[32,2,2,24,384]{4,3,2,1,0:T(8,128)(2,1)S(1)} %gather.3), channel_id=1, source_target_pairs={{0,32},{32,0},{1,33},{33,1},{2,34},{34,2},{3,35},{35,3},{4,36},{36... | collective-permute-start | bytes 7077896 | tf_op jit(solution)/shard_map/ppermute | solution.py:368

commit v7 on v6

--- a/solution.py
+++ b/solution.py
@@ -278,21 +278,19 @@
     def body(table_ref, scale_ref, kept_ref, got_ref, own_ref, other_ref, spectra_ref):
         core = lax.axis_index("core")
         slots = [table_ref[OWN_MEMBER + j] for j in range(2)]
-        for value in range(2):
-
-            @pl.when(core == value)
-            def _():
-                here = slice(value * width, (value + 1) * width)
-                there = slice((1 - value) * width, (2 - value) * width)
-                for j in range(2):
-                    for c in range(2):
-                        spectra_ref[j, c, :, here] = kept_ref[:, slots[j], c].reshape((size, width))
-                        spectra_ref[j, c, :, there] = got_ref[:, j, c].reshape((size, width))
-
-        for j in range(2):
-            spectra_ref[j, 2] = spectra_ref[j, 0] + spectra_ref[j, 1]
-        for j in range(2):
-            multiply(j, slots[j], scale_ref, spectra_ref, own_ref, other_ref)
+        def assemble(j):
+            for c in range(2):
+                kept = kept_ref[:, slots[j], c].reshape((size, width))
+                got = got_ref[:, j, c].reshape((size, width))
+                spectra_ref[j, c, :, :width] = jnp.where(core == 0, kept, got)
+                spectra_ref[j, c, :, width:] = jnp.where(core == 0, got, kept)
+
+        assemble(1)
+        assemble(0)
+        spectra_ref[1, 2] = spectra_ref[1, 0] + spectra_ref[1, 1]
+        multiply(0, slots[0], scale_ref, spectra_ref, own_ref, other_ref)
+        spectra_ref[0, 2] = spectra_ref[0, 0] + spectra_ref[0, 1]
+        multiply(1, slots[1], scale_ref, spectra_ref, own_ref, other_ref)
 
     return pl.pallas_call(
         body,
@@ -332,9 +330,12 @@
                 ).astype(jnp.bfloat16)
                 predicted[i, q] = traces[:, :time]
                 predicted[i, q + 1] = traces[:, time:]
-            target = out_ref.at[g, pl.ds(s * SUBLANES, SUBLANES), pl.ds(start, width)]
-            copies.append(pltpu.make_async_copy(predicted.at[i], target, out_sems.at[i]))
-            copies[-1].start()
+                if q % 4 == 2:
+                    source = predicted.at[i, pl.ds(q - 2, 4)]
+                    target = out_ref.at[g, pl.ds(s * SUBLANES + q - 2, 4), pl.ds(start, width)]
+                    sem = out_sems.at[len(copies)]
+                    copies.append(pltpu.make_async_copy(source, target, sem))
+                    copies[-1].start()
         for copy in copies:
             copy.wait()
 
@@ -352,7 +353,7 @@
         out_shape=jax.ShapeDtypeStruct((2, shots, 2 * width, time), jnp.bfloat16),
         scratch_shapes=[
             pltpu.VMEM((count * tiles, SUBLANES, width, time), jnp.bfloat16),
-            pltpu.SemaphoreType.DMA((count * tiles,)),
+            pltpu.SemaphoreType.DMA((2 * count * tiles,)),
         ],
         input_output_aliases=aliases,
         compiler_params=params(16),

time: 177 us -> 177 us (level)
  no operation moved by 1% of the time
where the time goes in v7:
time: 177 us
  blocking collectives  130 us (73%)
  Pallas kernels  30.3 us (17%)
  waiting for transfers between devices  9.44 us (5%)
  starting transfers between devices  6.78 us (4%)
    all_to_all x2, blocking collectives, exchange(): chunks = lax.all_to_all(chunks, COLUMN, 0, 0, tiled=True)  130 us
    pallas_call x1, Pallas kernels, chain(): pl.pallas_call(body, in_specs=[SMEM, VMEM, VMEM, VMEM], out_specs=[VMEM,...  12.8 us
    ppermute x4, waiting for transfers between devices, other_core(): return stay(lax.ppermute(part, 'core', [(0, 1), (1, 0)]))  9.44 us
    ppermute x4, starting transfers between devices, other_core(): return stay(lax.ppermute(part, 'core', [(0, 1), (1, 0)]))  6.78 us
    pallas_call x2, Pallas kernels, inverse_transform(): pl.pallas_call(body, in_specs=specs, out_specs=ANY, out_shape=jax.ShapeDt...  6.37 us
    pallas_call x1, Pallas kernels, forward_transform(): pl.pallas_call(body, in_specs=[HBM, HBM, SMEM, VMEM], out_specs=[VMEM, SM...  4.03 us
    pallas_call x1, Pallas kernels, forward_transform(): pl.pallas_call(body, in_specs=[HBM, HBM], out_specs=[VMEM, VMEM], out_sha...  4.01 us
  transfers between devices with their start and end apart: 4, of which 4 were waited for; matrix products, arithmetic and copies ran while one was open for 0% of the time, Pallas kernels for 4%

profile of v7, /device:TPU:1, one launch (start us, length us, event | category | flops | bytes accessed | tf_op | source)
XLA Modules:
  0.0 176.8 jit_solution(13212659793625133626)
XLA Ops:
  0.0 0.0 copy-start.2
  0.0 4.0 %forward.2 = (bf16[32,2,2,24,384]{4,3,2,1,0:T(8,128)(2,1)S(1)}, bf16[2,8,384,128]{3,2,1,0:T(8,128)(2,1)S(1)}) custom-call(bf16[64,128]{1,0:T(8,128)(2,1)} %constant.4.clone.forward_ref, bf16[2,24,768,128]{3,2,1,0:T(8,128)(2,1)} %records_ref.3), custom_call_target="tpu_custom_call" | custom-call | tf_op jit(solution)/shard_map/forward/pallas_call | solution.py:219
  4.0 1.5 collective-permute-start
  5.5 0.0 copy-done.2
  5.5 4.0 %forward.3 = (bf16[32,4,2,24,384]{4,3,2,1,0:T(8,128)(2,1)S(1)}, s32[8]{0:T(128)S(1)}) custom-call(bf16[64,128]{1,0:T(8,128)(2,1)} %constant.4.clone.forward_ref, bf16[2,24,768,128]{3,2,1,0:T(8,128)(2,1)} %records_ref.3, s32[8]{0:T(128)S(1)} %copy-done.2, bf16[2,8,384,128]{3,2,1,0:T(8,128)(2,1)S(1)} %get-tuple-element.11.refs_1_), custom_call_target="tpu_custom_call" | custom-call | tf_op jit(solution)/shard_map/forward/pallas_call | solution.py:228
  9.6 0.1 collective-permute-done.refs_0_
  9.7 0.8 scatter.2
  10.4 67.8 %all_to_all.10 = bf16[64,2,2,24,384]{4,3,2,1,0:T(8,128)(2,1)S(1)} all-to-all(bf16[64,2,2,24,384]{4,3,2,1,0:T(8,128)(2,1)S(1)} %bitcast.9), channel_id=1, replica_groups=mesh['zl'=2,'core'=2,'x'=4,'y'=4,'zh'=2] {'x','y','zh','zl'}, dimensions={0} | all-to-all | bytes 9437184 | tf_op jit(solution)/shard_map/all_to_all | solution.py:375
  78.2 0.0 copy-start.1
  78.2 0.7 gather.2
  79.0 2.5 %collective-permute-start.1 = (bf16[32,2,2,24,384]{4,3,2,1,0:T(8,128)(2,1)S(1)}, bf16[32,2,2,24,384]{4,3,2,1,0:T(8,128)(2,1)S(1)}, u32[]{:S(2)}, u32[]{:S(2)}) collective-permute-start(bf16[32,2,2,24,384]{4,3,2,1,0:T(8,128)(2,1)S(1)} %gather.2), channel_id=1, source_target_pairs={{0,32},{32,0},{1,33},{33,1},{2,34},{34,2},{3,35},{35,3},{4,36},{36... | collective-permute-start | bytes 7077896 | tf_op jit(solution)/shard_map/ppermute | solution.py:369
  81.5 4.2 %collective-permute-done.1.got_ref = bf16[32,2,2,24,384]{4,3,2,1,0:T(8,128)(2,1)S(1)} collective-permute-done((bf16[32,2,2,24,384]{4,3,2,1,0:T(8,128)(2,1)S(1)}, bf16[32,2,2,24,384]{4,3,2,1,0:T(8,128)(2,1)S(1)}, u32[]{:S(2)}, u32[]{:S(2)}) %collective-permute-start.1) | collective-permute-done | bytes 2359328 | tf_op jit(solution)/shard_map/ppermute | solution.py:369
  85.6 0.0 copy-done.1
  85.6 12.8 %chain.1 = (bf16[32,4,2,24,384]{4,3,2,1,0:T(8,128)(2,1)S(1)}, bf16[32,2,2,24,384]{4,3,2,1,0:T(8,128)(2,1)S(1)}) custom-call(s32[8]{0:T(128)S(1)} %get-tuple-element.12.table_ref, f32[1,768]{1,0:T(1,128)S(1)} %copy-done.1, bf16[32,4,2,24,384]{4,3,2,1,0:T(8,128)(2,1)S(1)} %bitcast.7, bf16[32,2,2,24,384]{4,3,2,1,0:T(8,128)(2,1)S(1)} %collective-permute-done.1.got_ref), custom_call_target="tpu_custom_call" | custom-call | tf_op jit(solution)/shard_map/chain/pallas_call | solution.py:295
  98.5 0.4 collective-permute-start.2
  98.9 4.2 %collective-permute-done.2.refs_0_ = bf16[32,2,2,24,384]{4,3,2,1,0:T(8,128)(2,1)S(1)} collective-permute-done((bf16[32,2,2,24,384]{4,3,2,1,0:T(8,128)(2,1)S(1)}, bf16[32,2,2,24,384]{4,3,2,1,0:T(8,128)(2,1)S(1)}, u32[]{:S(2)}, u32[]{:S(2)}) %collective-permute-start.2) | collective-permute-done | bytes 2359328 | tf_op jit(solution)/shard_map/ppermute | solution.py:369
  103.1 0.8 scatter.3
  103.9 62.3 %all_to_all.11 = bf16[64,2,2,24,384]{4,3,2,1,0:T(8,128)(2,1)S(1)} all-to-all(bf16[64,2,2,24,384]{4,3,2,1,0:T(8,128)(2,1)S(1)} %bitcast.8), channel_id=1, replica_groups=mesh['zl'=2,'core'=2,'x'=4,'y'=4,'zh'=2] {'x','y','zh','zl'}, dimensions={0} | all-to-all | bytes 9437184 | tf_op jit(solution)/shard_map/all_to_all | solution.py:375
  166.2 0.7 gather.3
  166.9 2.4 %collective-permute-start.3 = (bf16[32,2,2,24,384]{4,3,2,1,0:T(8,128)(2,1)S(1)}, bf16[32,2,2,24,384]{4,3,2,1,0:T(8,128)(2,1)S(1)}, u32[]{:S(2)}, u32[]{:S(2)}) collective-permute-start(bf16[32,2,2,24,384]{4,3,2,1,0:T(8,128)(2,1)S(1)} %gather.3), channel_id=1, source_target_pairs={{0,32},{32,0},{1,33},{33,1},{2,34},{34,2},{3,35},{35,3},{4,36},{36... | collective-permute-start | bytes 7077896 | tf_op jit(solution)/shard_map/ppermute | solution.py:369
  169.3 0.0 copy-done
  169.3 3.2 %inverse.2.refs_0_ = bf16[2,24,768,128]{3,2,1,0:T(8,128)(2,1)} custom-call(s32[8]{0:T(128)S(1)} %get-tuple-element.12.table_ref, bf16[64,128]{1,0:T(8,128)(2,1)S(1)} %copy-done, bf16[32,4,2,24,384]{4,3,2,1,0:T(8,128)(2,1)S(1)} %bitcast.5), custom_call_target="tpu_custom_call" | custom-call | tf_op jit(solution)/shard_map/inverse/pallas_call | solution.py:349
  172.5 1.0 collective-permute-done.3.total_ref
  173.5 3.2 %inverse.3 = bf16[2,24,768,128]{3,2,1,0:T(8,128)(2,1)} custom-call(s32[8]{0:T(128)S(1)} %get-tuple-element.12.table_ref, bf16[64,128]{1,0:T(8,128)(2,1)S(1)} %copy-done, bf16[32,2,2,24,384]{4,3,2,1,0:T(8,128)(2,1)S(1)} %collective-permute-done.3.total_ref, bf16[2,24,768,128]{3,2,1,0:T(8,128)(2,1)} %inverse.2.refs_0_), custom_call_target="tpu_custom_call", output_to_operand_aliasing={{}: (3, {})} | custom-call | tf_op jit(solution)/shard_map/inverse/pallas_call | solution.py:349
  (1 shorter events, 0.0 us)
Async XLA Ops:
  0.0 5.5 %copy-start.2 = (s32[8]{0:T(128)S(1)}, s32[8]{0:T(128)}, u32[]{:S(2)}) copy-start(s32[8]{0:T(128)} %refs_0_.1) | copy-start | bytes 100
  4.0 5.7 %collective-permute-start = (bf16[32,2,2,24,384]{4,3,2,1,0:T(8,128)(2,1)S(1)}, bf16[32,2,2,24,384]{4,3,2,1,0:T(8,128)(2,1)S(1)}, u32[]{:S(2)}, u32[]{:S(2)}) collective-permute-start(bf16[32,2,2,24,384]{4,3,2,1,0:T(8,128)(2,1)S(1)} %get-tuple-element.13), channel_id=1, source_target_pairs={{0,32},{32,0},{1,33},{33,1},{2,34},{34,2},{3,35},{35,3},{4,36},{36... | collective-permute-start | bytes 7077896 | tf_op jit(solution)/shard_map/ppermute | solution.py:369
  78.2 7.4 %copy-start.1 = (f32[1,768]{1,0:T(1,128)S(1)}, f32[1,768]{1,0:T(1,128)}, u32[]{:S(2)}) copy-start(f32[1,768]{1,0:T(1,128)} %scale_ref.1) | copy-start | bytes 9220
  79.0 6.7 %collective-permute-start.1 = (bf16[32,2,2,24,384]{4,3,2,1,0:T(8,128)(2,1)S(1)}, bf16[32,2,2,24,384]{4,3,2,1,0:T(8,128)(2,1)S(1)}, u32[]{:S(2)}, u32[]{:S(2)}) collective-permute-start(bf16[32,2,2,24,384]{4,3,2,1,0:T(8,128)(2,1)S(1)} %gather.2), channel_id=1, source_target_pairs={{0,32},{32,0},{1,33},{33,1},{2,34},{34,2},{3,35},{35,3},{4,36},{36... | collective-permute-start | bytes 7077896 | tf_op jit(solution)/shard_map/ppermute | solution.py:369
  98.5 4.6 %collective-permute-start.2 = (bf16[32,2,2,24,384]{4,3,2,1,0:T(8,128)(2,1)S(1)}, bf16[32,2,2,24,384]{4,3,2,1,0:T(8,128)(2,1)S(1)}, u32[]{:S(2)}, u32[]{:S(2)}) collective-permute-start(bf16[32,2,2,24,384]{4,3,2,1,0:T(8,128)(2,1)S(1)} %get-tuple-element.15), channel_id=1, source_target_pairs={{0,32},{32,0},{1,33},{33,1},{2,34},{34,2},{3,35},{35,3},{4,36},{36... | collective-permute-start | bytes 7077896 | tf_op jit(solution)/shard_map/ppermute | solution.py:369
  166.2 3.1 %copy-start = (bf16[64,128]{1,0:T(8,128)(2,1)S(1)}, bf16[64,128]{1,0:T(8,128)(2,1)}, u32[]{:S(2)}) copy-start(bf16[64,128]{1,0:T(8,128)(2,1)} %constant.5.clone.inverse_ref) | copy-start | bytes 49156
  166.9 6.6 %collective-permute-start.3 = (bf16[32,2,2,24,384]{4,3,2,1,0:T(8,128)(2,1)S(1)}, bf16[32,2,2,24,384]{4,3,2,1,0:T(8,128)(2,1)S(1)}, u32[]{:S(2)}, u32[]{:S(2)}) collective-permute-start(bf16[32,2,2,24,384]{4,3,2,1,0:T(8,128)(2,1)S(1)} %gather.3), channel_id=1, source_target_pairs={{0,32},{32,0},{1,33},{33,1},{2,34},{34,2},{3,35},{35,3},{4,36},{36... | collective-permute-start | bytes 7077896 | tf_op jit(solution)/shard_map/ppermute | solution.py:369
